TPU v7x, 32 devices: a whole 2x2x4 slice. The times are simulated.
32 devices in a mesh: ctx: 4 (over y, x), exp: 8 (over z, core).
Axes of the slice: x: 2, y: 2, z: 4, core: 2. Of those that a mesh axis runs over, the one named last changes fastest.
Arguments:
- states: bfloat16 [8, 128, 2560], P('exp'), may hold values from -13 to 13
- out_grad: bfloat16 [8, 128, 2560], P('exp'), may hold values from -6 to 6
- doc_keys: bfloat16 [8, 512, 2560], P('exp', 'ctx'), may hold values from -60 to 60
- doc_values: bfloat16 [8, 512, 2560], P('exp', 'ctx'), may hold values from -18 to 18
- norm_gain: float32 [2560], replicated, may hold values from 0.5 to 1.5
- expert_ids: int32 [8, 128, 2], P('exp'), may hold values from 0 to 7, all different within a row; in each aligned block of 128 rows (0 to 127, 128 to 255, ..., all dimensions but the last counted through in order) at most 40 rows name the same one
- gate_values: float32 [8, 128, 2], P('exp'), may hold values from 0.5 to 2.5
- expert_weights: bfloat16 [8, 2048, 2, 2560], P('exp', 'ctx'), may hold values from -0.125 to 0.125
Outputs:
- states_grad: bfloat16 [8, 128, 2560], P('exp')
- keys_grad: bfloat16 [8, 512, 2560], P('exp', 'ctx')
- values_grad: bfloat16 [8, 512, 2560], P('exp', 'ctx')
- weights_grad: bfloat16 [8, 2048, 2, 2560], P('exp', 'ctx')
Inputs may be any that keep to these rules, and one draw needn't show every extreme that they name: `expert_ids`: within one sequence's 128 tokens, every expert is named by at most 40 tokens.
All inputs are finite; a program needn't handle non-finite values.
Results may differ from a plain program's by a relative error of at most 0.04.
Values may be sent and summed in bfloat16 or wider, within the bound.
A program may use at most 128 MiB of HBM per device.

v0:
```python
import jax
import jax.numpy as jnp
from jax import lax
from jax.sharding import PartitionSpec as P

HEADS = 20
HEAD = 128
TOP = 2


EPSILON = 1e-05


def joined(value, axis, join):
    pieces = jax.tree.map(lambda part: lax.all_gather(part, axis), value)
    head = jax.tree.map(lambda part: part[0], pieces)
    tail = jax.tree.map(lambda part: part[1:], pieces)
    running, _ = lax.scan(lambda running, share: (join(running, share), None), head, tail)
    return running


def combine_scores(one_side, other_side):
    top_score = jnp.maximum(one_side[0], other_side[0])
    factor_one = jnp.exp(one_side[0] - top_score)
    factor_two = jnp.exp(other_side[0] - top_score)
    summed = one_side[1] * factor_one + other_side[1] * factor_two
    weighted = one_side[2] * factor_one + other_side[2] * factor_two
    return (top_score, summed, weighted)


def on_device(
    states, out_grad, doc_keys, doc_values, norm_gain, expert_ids, gate_values, expert_weights
):
    tokens = states.shape[1]
    model_width = states.shape[2]
    key_count = doc_keys.shape[1]
    scale = HEAD ** (-0.5)
    inputs = states[0].astype(jnp.float32)
    inverse = lax.rsqrt(jnp.mean(inputs * inputs, axis=-1, keepdims=True) + EPSILON)
    unit = inputs * inverse
    normed = (unit * norm_gain).astype(jnp.bfloat16)
    upstream = out_grad[0]
    queries = normed.reshape(tokens, HEADS, HEAD)
    key_heads = doc_keys[0].reshape(key_count, HEADS, HEAD)
    value_heads = doc_values[0].reshape(key_count, HEADS, HEAD)
    grad_heads = upstream.reshape(tokens, HEADS, HEAD)
    scores = (
        jnp.einsum("qhd,khd->hqk", queries, key_heads, preferred_element_type=jnp.float32) * scale
    )
    local_peak = jnp.max(scores, axis=-1)
    local_weights = jnp.exp(scores - local_peak[..., None])
    local_total = jnp.sum(local_weights, axis=-1)
    slopes = jnp.einsum("qhd,khd->hqk", grad_heads, value_heads, preferred_element_type=jnp.float32)
    local_inner = jnp.sum(local_weights * slopes, axis=-1)
    peak, total, merged = joined((local_peak, local_total, local_inner), "ctx", combine_scores)
    delta = merged / total
    probs = jnp.exp(scores - peak[..., None]) / total[..., None]
    score_grad = (probs * (slopes - delta[..., None])).astype(jnp.bfloat16)
    probs_low = probs.astype(jnp.bfloat16)
    values_grad = jnp.einsum(
        "hqk,qhd->khd", probs_low, grad_heads, preferred_element_type=jnp.float32
    )
    keys_grad = (
        jnp.einsum("hqk,qhd->khd", score_grad, queries, preferred_element_type=jnp.float32) * scale
    )
    query_grad = (
        jnp.einsum(
            "hqk,khd->qhd", score_grad, key_heads, preferred_element_type=jnp.float32
        ).reshape(tokens, model_width)
        * scale
    )
    ctx_count = lax.axis_size("ctx")
    expert_count = lax.axis_size("exp")
    capacity = ctx_count * (
        (5 * TOP * tokens + 4 * expert_count * ctx_count - 1) // (4 * expert_count * ctx_count)
    )
    assigned = tokens * TOP
    flat_ids = expert_ids[0].reshape(assigned)
    onehot = (flat_ids[:, None] == jnp.arange(expert_count, dtype=jnp.int32)[None, :]).astype(
        jnp.int32
    )
    earlier = jnp.cumsum(onehot, axis=0) - onehot
    slot = jnp.sum(earlier * onehot, axis=1)
    placed = flat_ids * capacity + slot
    table = (
        jnp.full((expert_count * capacity,), assigned, jnp.int32)
        .at[placed]
        .set(jnp.arange(assigned, dtype=jnp.int32))
    )
    filled = table < assigned
    safe_index = jnp.minimum(table, assigned - 1)
    source = safe_index // TOP
    slot_gate = jnp.where(filled, gate_values[0].reshape(assigned)[safe_index], 0.0)
    send_rows = jnp.where(filled[:, None], normed[source], jnp.zeros((), jnp.bfloat16))
    send_rows = send_rows.reshape(expert_count, capacity, model_width)
    send_grads = (slot_gate[:, None] * upstream[source].astype(jnp.float32)).astype(jnp.bfloat16)
    send_grads = send_grads.reshape(expert_count, capacity, model_width)
    got_rows, got_grads = (
        lax.all_to_all(send_rows, "exp", split_axis=0, concat_axis=0, tiled=True),
        lax.all_to_all(send_grads, "exp", split_axis=0, concat_axis=0, tiled=True),
    )
    slot_rows = got_rows.shape[0] * got_rows.shape[1]
    rows = got_rows.reshape(slot_rows, model_width)
    douts = got_grads.reshape(slot_rows, model_width)
    w_in = expert_weights[0, :, 0, :]
    w_out = expert_weights[0, :, 1, :]
    pre = jnp.einsum("sd,hd->sh", rows, w_in, preferred_element_type=jnp.float32)
    activ, pull = jax.vjp(jax.nn.gelu, pre)
    activ_low = activ.astype(jnp.bfloat16)
    act_grad = jnp.einsum("sd,hd->sh", douts, w_out, preferred_element_type=jnp.float32)
    pre_grad = pull(act_grad)[0].astype(jnp.bfloat16)
    grad_in = jnp.einsum("sh,sd->hd", pre_grad, rows, preferred_element_type=jnp.float32)
    grad_proj = jnp.einsum("sh,sd->hd", activ_low, douts, preferred_element_type=jnp.float32)
    weights_grad = jnp.stack([grad_in, grad_proj], axis=1).astype(jnp.bfloat16)[None]
    partial_rows = jnp.einsum("sh,hd->sd", pre_grad, w_in, preferred_element_type=jnp.float32)
    partial_rows = partial_rows.astype(jnp.bfloat16).reshape(got_rows.shape)
    returned = lax.all_to_all(partial_rows, "exp", split_axis=0, concat_axis=0, tiled=True)
    picked_rows = returned.reshape(expert_count * capacity, model_width)[placed]
    moe_part = jnp.sum(picked_rows.astype(jnp.float32).reshape(tokens, TOP, model_width), axis=1)
    total_grad = lax.psum((query_grad + moe_part).astype(jnp.bfloat16), "ctx").astype(jnp.float32)
    scaled = total_grad * norm_gain
    states_grad = upstream.astype(jnp.float32) + inverse * (
        scaled - unit * jnp.mean(scaled * unit, axis=-1, keepdims=True)
    )
    return (
        states_grad.astype(jnp.bfloat16)[None],
        keys_grad.reshape(key_count, model_width).astype(jnp.bfloat16)[None],
        values_grad.reshape(key_count, model_width).astype(jnp.bfloat16)[None],
        weights_grad,
    )


def solution(mesh):
    return jax.shard_map(
        on_device,
        mesh=mesh,
        in_specs=(
            P("exp", None, None),
            P("exp", None, None),
            P("exp", "ctx", None),
            P("exp", "ctx", None),
            P(),
            P("exp", None, None),
            P("exp", None, None),
            P("exp", "ctx", None, None),
        ),
        out_specs=(
            P("exp", None, None),
            P("exp", "ctx", None),
            P("exp", "ctx", None),
            P("exp", "ctx", None, None),
        ),
        check_vma=False,
    )
```

profile of v0, /device:TPU:0, one launch (start us, length us, event | category | flops | bytes accessed | tf_op | source)
XLA Modules:
  0.0 229.4 jit_solution(10923830295777130794)
XLA Ops:
  7.2 0.7 broadcast_multiply_fusion
  7.8 0.8 copy.59
  8.9 1.3 fusion.8
  11.5 1.4 scatter_custom_fusion
  12.9 0.8 copy.61
  13.8 2.5 %gather_fusion = f32[320]{0:T(512)S(1)} fusion(f32[256]{0:T(256)S(1)} %reshape_squeeze.16, s32[1024]{0:T(1024)S(1)} %get-tuple-element.86), kind=kCustom, calls=%fused_computation | custom fusion | bytes 3840 | tf_op jit(solution)/shard_map/gather | solution.py:93
  16.6 2.6 %gather_fusion.2 = bf16[320,2560]{1,0:T(8,128)(2,1)S(1)} fusion(bf16[128,2560]{1,0:T(8,128)(2,1)S(1)} %multiply_convert_fusion, s32[1024]{0:T(1024)S(1)} %get-tuple-element.85), kind=kCustom, calls=%fused_computation.2 | custom fusion | bytes 3278080 | tf_op jit(solution)/shard_map/gather | solution.py:94
  19.3 1.3 broadcast_select_fusion
  20.6 6.4 %all-to-all-start.1 = ((bf16[8,40,2560]{2,1,0:T(8,128)(2,1)}), bf16[8,40,2560]{2,1,0:T(8,128)(2,1)}, u32[]{:S(2)}, u32[]{:S(2)}) async-start(bf16[8,40,2560]{2,1,0:T(8,128)(2,1)} %broadcast_select_fusion), calls=%async_computation.1 | async-start | bytes 3276800 | tf_op jit(solution)/shard_map/all_to_all | solution.py:99
  27.3 1.8 copy.50
  29.1 2.4 %copy.54 = bf16[1,128,2560]{1,2,0:T(8,128)(2,1)} copy(bf16[1,128,2560]{2,1,0:T(8,128)(2,1)} %param.13) | data formatting | bytes 1310720 | tf_op args[3]
  31.5 1.1 copy.53
  32.6 3.2 %gather_fusion.1 = bf16[320,2560]{1,0:T(8,128)(2,1)} fusion(bf16[128,2560]{1,0:T(8,128)(2,1)S(1)} %bitcast.108, s32[1024]{0:T(1024)S(1)} %get-tuple-element.85), kind=kCustom, calls=%fused_computation.1 | custom fusion | bytes 3278080 | tf_op jit(solution)/shard_map/gather | solution.py:96
  35.8 0.8 fusion.37
  36.6 8.2 %all-gather.3 = f32[4,20,128]{2,1,0:T(8,128)S(1)} all-gather(f32[1,20,128]{2,1,0:T(8,128)S(1)} %bitcast.127), channel_id=2, replica_groups=mesh['ctx'=4,'exp'=8] {'ctx'}, dimensions={0}, use_global_device_ids=true | all-gather | bytes 51200 | tf_op jit(solution)/shard_map/all_gather | solution.py:15
  44.9 1.5 multiply_reduce_fusion.1
  46.4 8.2 %all-gather.4 = f32[4,20,128]{2,1,0:T(8,128)S(1)} all-gather(f32[1,20,128]{2,1,0:T(8,128)S(1)} %bitcast.129), channel_id=3, replica_groups=mesh['ctx'=4,'exp'=8] {'ctx'}, dimensions={0}, use_global_device_ids=true | all-gather | bytes 51200 | tf_op jit(solution)/shard_map/all_gather | solution.py:15
  54.6 7.2 %all-gather.5 = f32[4,20,128]{2,1,0:T(8,128)S(1)} all-gather(f32[1,20,128]{2,1,0:T(8,128)S(1)} %bitcast.128), channel_id=4, replica_groups=mesh['ctx'=4,'exp'=8] {'ctx'}, dimensions={0}, use_global_device_ids=true | all-gather | bytes 51200 | tf_op jit(solution)/shard_map/all_gather | solution.py:15
  61.8 1.6 fusion.5
  63.4 2.9 %all-to-all-done.1 = bf16[8,40,2560]{2,1,0:T(8,128)(2,1)} async-done(((bf16[8,40,2560]{2,1,0:T(8,128)(2,1)}), bf16[8,40,2560]{2,1,0:T(8,128)(2,1)}, u32[]{:S(2)}, u32[]{:S(2)}) %all-to-all-start.1) | async-done | bytes 1638432 | tf_op jit(solution)/shard_map/all_to_all | solution.py:99
  66.3 3.8 %all-to-all-start = ((bf16[8,40,2560]{2,1,0:T(8,128)(2,1)}), bf16[8,40,2560]{2,1,0:T(8,128)(2,1)S(1)}, u32[]{:S(2)}, u32[]{:S(2)}) async-start(bf16[8,40,2560]{2,1,0:T(8,128)(2,1)} %fusion.5), calls=%async_computation | async-start | bytes 3276800 | tf_op jit(solution)/shard_map/all_to_all | solution.py:100
  70.1 11.3 %fusion.36 = (bf16[1,512,1,2560]{3,2,1,0:T(2,128)(2,1)}, bf16[1,512,1,2560]{3,2,1,0:T(2,128)(2,1)S(1)}) fusion(bf16[1,512,2,2560]{3,2,1,0:T(2,128)(2,1)} %param.17), kind=kLoop, calls=%fused_computation.96 | loop fusion | bytes 10485760 | tf_op jit(solution)/shard_map/slice | solution.py:106
  81.4 2.3 copy-done.8
  83.7 3.3 %fusion.11 = f32[320,512]{1,0:T(8,128)} fusion(bf16[320,2560]{1,0:T(8,128)(2,1)} %bitcast.26, bf16[1,512,1,2560]{3,2,1,0:T(2,128)(2,1)S(1)} %get-tuple-element.79), kind=kOutput, calls=%fused_computation.45 | convolution fusion | flops 838860800 | bytes 4915200 | tf_op jit(solution)/shard_map/sd,hd->sh/dot_general | solution.py:107
  87.0 22.0 %all-to-all-done = bf16[8,40,2560]{2,1,0:T(8,128)(2,1)S(1)} async-done(((bf16[8,40,2560]{2,1,0:T(8,128)(2,1)}), bf16[8,40,2560]{2,1,0:T(8,128)(2,1)S(1)}, u32[]{:S(2)}, u32[]{:S(2)}) %all-to-all-start) | async-done | bytes 1638432 | tf_op jit(solution)/shard_map/all_to_all | solution.py:100
  109.0 4.6 %fusion.18 = bf16[320,512]{1,0:T(8,128)(2,1)S(1)} fusion(f32[320,512]{1,0:T(8,128)} %fusion.11, bf16[320,2560]{1,0:T(8,128)(2,1)S(1)} %bitcast.121, bf16[1,512,1,2560]{3,2,1,0:T(2,128)(2,1)} %get-tuple-element.78), kind=kOutput, calls=%fused_computation.54 | convolution fusion | flops 842137600 | bytes 5242880 | tf_op jit(solution)/shard_map/sd,hd->sh/dot_general | solution.py:110
  113.8 2.2 convolution_convert_fusion.2
  116.0 3.7 %all-to-all-start.2 = ((bf16[8,40,2560]{2,1,0:T(8,128)(2,1)}), bf16[8,40,2560]{2,1,0:T(8,128)(2,1)S(1)}, u32[]{:S(2)}, u32[]{:S(2)}) async-start(bf16[8,40,2560]{2,1,0:T(8,128)(2,1)} %bitcast.123), calls=%async_computation.2 | async-start | bytes 3276800 | tf_op jit(solution)/shard_map/all_to_all | solution.py:117
  120.1 2.1 multiply_convert_fusion.1
  122.3 1.4 convolution_multiply_fusion
  123.6 2.8 %copy.64 = f32[128,2560]{1,0:T(8,128)} copy(f32[128,2560]{0,1:T(8,128)} %bitcast.116) | data formatting | bytes 2621440 | tf_op jit(solution)/shard_map/mul | solution.py:67
  126.4 3.0 %fusion.9 = bf16[128,20,128]{2,0,1:T(8,128)(2,1)} fusion(bf16[20,128,128]{1,2,0:T(8,128)(2,1)} %copy-done.5, f32[128,20,128]{0,2,1:T(8,128)} %bitcast.111, f32[20,128]{1,0:T(8,128)S(1)} %bitcast.126, f32[128]{0:T(128)S(1)} %add_rsqrt_fusion), kind=kOutput, calls=%fused_computation.43 | convolution fusion | flops 85524480 | bytes 2632192 | tf_op jit(solution)/shard_map/hqk,qhd->khd/dot_general | solution.py:64
  129.4 2.2 copy.67
  131.5 2.2 copy.69
  133.7 2.9 %convolution_convert_fusion.3 = bf16[20,128,128]{1,2,0:T(8,128)(2,1)} fusion(bf16[128,20,128]{0,2,1:T(8,128)(2,1)} %bitcast.117, f32[20,128,128]{1,2,0:T(8,128)} %copy-done.2, f32[20,128]{1,0:T(8,128)S(1)} %get-tuple-element.44, f32[20,128]{1,0:T(8,128)S(1)} %get-tuple-element.43), kind=kOutput, calls=%fused_computation.29 | convolution fusion | flops 85196800 | bytes 2641920 | tf_op jit(solution)/shard_map/hqk,qhd->khd/dot_general | solution.py:60
  136.6 2.2 copy.70
  138.8 4.8 %fusion.4 = bf16[1,512,1,2560]{3,1,2,0:T(8,128)(2,1)} fusion(bf16[320,2560]{1,0:T(8,128)(2,1)} %bitcast.122, f32[320,512]{1,0:T(8,128)} %fusion.11), kind=kOutput, calls=%fused_computation.17 | convolution fusion | flops 841646080 | bytes 4915200 | tf_op jit(solution)/shard_map/sh,sd->hd/dot_general | solution.py:113
  143.5 15.3 %all-to-all-done.2 = bf16[8,40,2560]{2,1,0:T(8,128)(2,1)S(1)} async-done(((bf16[8,40,2560]{2,1,0:T(8,128)(2,1)}), bf16[8,40,2560]{2,1,0:T(8,128)(2,1)S(1)}, u32[]{:S(2)}, u32[]{:S(2)}) %all-to-all-start.2) | async-done | bytes 1638432 | tf_op jit(solution)/shard_map/all_to_all | solution.py:117
  158.9 2.5 %gather_fusion.3 = bf16[256,2560]{1,0:T(8,128)(2,1)} fusion(bf16[320,2560]{1,0:T(8,128)(2,1)S(1)} %bitcast.109, s32[1024]{0:T(1024)S(1)} %pad_clamp_fusion), kind=kCustom, calls=%fused_computation.3 | custom fusion | bytes 2622464 | tf_op jit(solution)/shard_map/gather | solution.py:118
  161.4 4.1 %reshape.188 = f32[128,2,2560]{2,1,0:T(2,128)} reshape(bf16[256,2560]{1,0:T(8,128)(2,1)} %gather_fusion.3) | data formatting | bytes 3932160 | tf_op jit(solution)/shard_map/convert_element_type | solution.py:119
  165.5 6.0 %reduce_sum.61 = f32[128,2560]{1,0:T(8,128)} reduce(f32[128,2,2560]{2,1,0:T(2,128)} %reshape.188, f32[]{:T(128)} %constant.26.clone.1), dimensions={1}, to_apply=%region_10.11 | reduce | flops 327680 | bytes 3932164 | tf_op jit(solution)/shard_map/reduce_sum | solution.py:119
  171.5 2.3 %add_convert_fusion.1 = bf16[128,2560]{1,0:T(8,128)(2,1)} fusion(f32[128,2560]{1,0:T(8,128)S(1)} %copy-done.10, f32[128,2560]{1,0:T(8,128)} %reduce_sum.61), kind=kLoop, calls=%fused_computation.36 | loop fusion | flops 655360 | bytes 3276800 | tf_op jit(solution)/shard_map/convert_element_type | solution.py:120
  173.9 3.1 %fusion.3 = bf16[1,512,1,2560]{3,1,2,0:T(8,128)(2,1)S(1)} fusion(bf16[320,512]{1,0:T(8,128)(2,1)S(1)} %copy-done.21, bf16[320,2560]{1,0:T(8,128)(2,1)} %bitcast.26), kind=kOutput, calls=%fused_computation.16 | convolution fusion | flops 840171520 | bytes 4587520 | tf_op jit(solution)/shard_map/sh,sd->hd/dot_general | solution.py:112
  177.0 2.7 %pad_maximum_fusion = bf16[1,512,2,2560]{3,1,2,0:T(8,128)(2,1)} fusion(bf16[1,512,1,2560]{3,1,2,0:T(8,128)(2,1)S(1)} %copy-done.11, bf16[1,512,1,2560]{3,1,2,0:T(8,128)(2,1)S(1)} %fusion.3), kind=kLoop, calls=%fused_computation.13 | loop fusion | flops 2621440 | bytes 10485760 | tf_op jit(solution)/shard_map/stack | solution.py:114
  179.7 10.2 %copy.71 = bf16[1,512,2,2560]{3,2,1,0:T(2,128)(2,1)} copy(bf16[1,512,2,2560]{3,1,2,0:T(8,128)(2,1)} %pad_maximum_fusion) | data formatting | bytes 10485760
  190.0 29.7 %all-reduce.2.cloned.1.call-done = bf16[128,2560]{1,0:T(8,128)(2,1)} async-done(((bf16[128,2560]{1,0:T(8,128)(2,1)}), bf16[128,2560]{1,0:T(8,128)(2,1)}) %all-reduce.2.cloned.1.call-update) | async-done | bytes 655376 | tf_op jit(solution)/shard_map/psum | solution.py:120
  219.7 1.5 multiply_reduce_fusion
  221.2 1.3 fusion.19
  (88 shorter events, 3.0 us)
Async XLA Ops:
  10.2 6.2 %copy-start.1 = (bf16[1,128,2560]{2,1,0:T(8,128)(2,1)S(1)}, bf16[1,128,2560]{2,1,0:T(8,128)(2,1)}, u32[]{:S(2)}) copy-start(bf16[1,128,2560]{2,1,0:T(8,128)(2,1)} %param.10) | copy-start | bytes 1966084
  10.2 6.2 %copy-start.17 = (f32[2560]{0:T(1024)S(1)}, f32[2560]{0:T(1024)}, u32[]{:S(2)}) copy-start(f32[2560]{0:T(1024)} %param.14) | copy-start | bytes 30724
  20.6 45.7 %all-to-all-start.1 = ((bf16[8,40,2560]{2,1,0:T(8,128)(2,1)}), bf16[8,40,2560]{2,1,0:T(8,128)(2,1)}, u32[]{:S(2)}, u32[]{:S(2)}) async-start(bf16[8,40,2560]{2,1,0:T(8,128)(2,1)} %broadcast_select_fusion), calls=%async_computation.1 | async-start | bytes 3276800 | tf_op jit(solution)/shard_map/all_to_all | solution.py:99
  27.2 8.6 %copy-start.3 = (f32[1,128,2560]{1,2,0:T(8,128)}, f32[1,128,2560]{1,2,0:T(8,128)S(1)}, u32[]{:S(2)}) copy-start(f32[1,128,2560]{1,2,0:T(8,128)S(1)} %copy.49) | copy-start | bytes 3932164
  27.3 4.2 %copy-start = (bf16[1,128,2560]{2,1,0:T(8,128)(2,1)S(1)}, bf16[1,128,2560]{2,1,0:T(8,128)(2,1)}, u32[]{:S(2)}) copy-start(bf16[1,128,2560]{2,1,0:T(8,128)(2,1)} %param.11) | copy-start | bytes 1966084
  29.1 6.7 %copy-start.6 = (bf16[1,128,2560]{1,2,0:T(8,128)(2,1)}, bf16[1,128,2560]{1,2,0:T(8,128)(2,1)S(1)}, u32[]{:S(2)}) copy-start(bf16[1,128,2560]{1,2,0:T(8,128)(2,1)S(1)} %copy.50) | copy-start | bytes 1966084
  35.8 9.1 %copy-start.12 = (bf16[1,128,2560]{1,2,0:T(8,128)(2,1)S(1)}, bf16[1,128,2560]{1,2,0:T(8,128)(2,1)}, u32[]{:S(2)}) copy-start(bf16[1,128,2560]{1,2,0:T(8,128)(2,1)} %copy.53) | copy-start | bytes 1966084
  35.8 9.1 %copy-start.13 = (bf16[1,128,2560]{1,2,0:T(8,128)(2,1)S(1)}, bf16[1,128,2560]{1,2,0:T(8,128)(2,1)}, u32[]{:S(2)}) copy-start(bf16[1,128,2560]{1,2,0:T(8,128)(2,1)} %copy.54) | copy-start | bytes 1966084
  36.6 9.8 %copy-start.2 = (f32[20,128,128]{1,2,0:T(8,128)}, f32[20,128,128]{1,2,0:T(8,128)S(1)}, u32[]{:S(2)}) copy-start(f32[20,128,128]{1,2,0:T(8,128)S(1)} %get-tuple-element.83) | copy-start | bytes 3932164
  44.8 25.2 %copy-start.16 = (f32[4,20,128]{2,1,0:T(8,128)}, f32[4,20,128]{2,1,0:T(8,128)S(1)}, u32[]{:S(2)}) copy-start(f32[4,20,128]{2,1,0:T(8,128)S(1)} %all-gather.3) | copy-start | bytes 122884
  44.9 17.0 %copy-start.4 = (bf16[320,2560]{1,0:T(8,128)(2,1)S(1)}, bf16[320,2560]{1,0:T(8,128)(2,1)}, u32[]{:S(2)}) copy-start(bf16[320,2560]{1,0:T(8,128)(2,1)} %gather_fusion.1) | copy-start | bytes 4915204
  54.6 15.4 %copy-start.18 = (f32[4,20,128]{2,1,0:T(8,128)}, f32[4,20,128]{2,1,0:T(8,128)S(1)}, u32[]{:S(2)}) copy-start(f32[4,20,128]{2,1,0:T(8,128)S(1)} %all-gather.4) | copy-start | bytes 122884
  61.8 8.3 %copy-start.19 = (f32[4,20,128]{2,1,0:T(8,128)}, f32[4,20,128]{2,1,0:T(8,128)S(1)}, u32[]{:S(2)}) copy-start(f32[4,20,128]{2,1,0:T(8,128)S(1)} %all-gather.5) | copy-start | bytes 122884
  66.3 42.7 %all-to-all-start = ((bf16[8,40,2560]{2,1,0:T(8,128)(2,1)}), bf16[8,40,2560]{2,1,0:T(8,128)(2,1)S(1)}, u32[]{:S(2)}, u32[]{:S(2)}) async-start(bf16[8,40,2560]{2,1,0:T(8,128)(2,1)} %fusion.5), calls=%async_computation | async-start | bytes 3276800 | tf_op jit(solution)/shard_map/all_to_all | solution.py:100
  81.4 2.3 %copy-start.8 = (bf16[1,512,1,2560]{3,2,1,0:T(2,128)(2,1)}, bf16[1,512,1,2560]{3,2,1,0:T(2,128)(2,1)S(1)}, u32[]{:S(2)}) copy-start(bf16[1,512,1,2560]{3,2,1,0:T(2,128)(2,1)S(1)} %get-tuple-element.79) | copy-start | bytes 7864324
  109.0 4.6 %copy-start.15 = (bf16[8,40,2560]{2,1,0:T(8,128)(2,1)}, bf16[8,40,2560]{2,1,0:T(8,128)(2,1)S(1)}, u32[]{:S(2)}) copy-start(bf16[8,40,2560]{2,1,0:T(8,128)(2,1)S(1)} %all-to-all-done) | copy-start | bytes 4915204
  109.0 4.8 %copy-start.9 = (bf16[1,512,1,2560]{3,2,1,0:T(2,128)(2,1)S(1)}, bf16[1,512,1,2560]{3,2,1,0:T(2,128)(2,1)}, u32[]{:S(2)}) copy-start(bf16[1,512,1,2560]{3,2,1,0:T(2,128)(2,1)} %copy-done.8) | copy-start | bytes 7864324
  113.8 2.2 copy-start.20
  116.0 3.8 %slice-start = ((f32[4,20,128]{2,1,0:T(8,128)}), f32[3,20,128]{2,1,0:T(8,128)S(1)}, s32[]{:S(2)}) async-start(f32[4,20,128]{2,1,0:T(8,128)} %copy-done.16), calls=%async_computation.4 | async-start | bytes 73728 | tf_op jit(solution)/shard_map/slice | solution.py:17
  116.0 3.8 %slice-start.1 = ((f32[4,20,128]{2,1,0:T(8,128)}), f32[3,20,128]{2,1,0:T(8,128)S(1)}, s32[]{:S(2)}) async-start(f32[4,20,128]{2,1,0:T(8,128)} %copy-done.18), calls=%async_computation.5 | async-start | bytes 73728 | tf_op jit(solution)/shard_map/slice | solution.py:17
  116.0 3.8 %slice-start.2 = ((f32[4,20,128]{2,1,0:T(8,128)}), f32[3,20,128]{2,1,0:T(8,128)S(1)}, s32[]{:S(2)}) async-start(f32[4,20,128]{2,1,0:T(8,128)} %copy-done.19), calls=%async_computation.6 | async-start | bytes 73728 | tf_op jit(solution)/shard_map/slice | solution.py:17
  116.0 42.9 %all-to-all-start.2 = ((bf16[8,40,2560]{2,1,0:T(8,128)(2,1)}), bf16[8,40,2560]{2,1,0:T(8,128)(2,1)S(1)}, u32[]{:S(2)}, u32[]{:S(2)}) async-start(bf16[8,40,2560]{2,1,0:T(8,128)(2,1)} %bitcast.123), calls=%async_computation.2 | async-start | bytes 3276800 | tf_op jit(solution)/shard_map/all_to_all | solution.py:117
  119.7 99.9 %all-reduce.2.cloned.1.call-start = ((), (), s32[]{:S(2)}) async-start(), calls=%async_computation.3 | async-start | bytes 1310720 | tf_op jit(solution)/shard_map/psum | solution.py:120
  120.1 2.2 copy-start.7
  122.2 1.4 copy-start.5
  165.5 6.0 %copy-start.10 = (f32[128,2560]{1,0:T(8,128)S(1)}, f32[128,2560]{1,0:T(8,128)}, u32[]{:S(2)}) copy-start(f32[128,2560]{1,0:T(8,128)} %copy.64) | copy-start | bytes 3932164
  171.5 2.4 %copy-start.21 = (bf16[320,512]{1,0:T(8,128)(2,1)S(1)}, bf16[320,512]{1,0:T(8,128)(2,1)}, u32[]{:S(2)}) copy-start(bf16[320,512]{1,0:T(8,128)(2,1)} %copy-done.20) | copy-start | bytes 983044
  173.8 3.1 %copy-start.11 = (bf16[1,512,1,2560]{3,1,2,0:T(8,128)(2,1)S(1)}, bf16[1,512,1,2560]{3,1,2,0:T(8,128)(2,1)}, u32[]{:S(2)}) copy-start(bf16[1,512,1,2560]{3,1,2,0:T(8,128)(2,1)} %fusion.4) | copy-start | bytes 7864324
  219.7 1.6 copy-start.14
Sparse Core Ops, SparseCore 0:
  174.0 45.6 all-reduce.1
where the time goes:
time: 230 us; the launch traced here: 229 us
  waiting for transfers between devices  69.9 us (30%)
  local copies, waits for them, and re-layouts  57.8 us (25%)
  matrix products  27.6 us (12%)
  blocking collectives  23.7 us (10%)
  other arithmetic  22.1 us (10%)
  between operations  14.4 us (6%)
  starting transfers between devices  13.9 us (6%)
    psum x1, waiting for transfers between devices, on_device(): lax.psum((query_grad + moe_part).astype(jnp.bfloat16), 'ctx')  29.7 us
    unnamed x52, local copies, waits for them, and re-layouts  24 us
    all_gather x3, blocking collectives, joined(): pieces = jax.tree.map(lambda part: lax.all_gather(part, axis), value)  23.7 us
    all_to_all x1, waiting for transfers between devices, on_device(): lax.all_to_all(send_grads, 'exp', split_axis=0, concat_axis=0, tiled=True)  22 us
    all_to_all x1, waiting for transfers between devices, on_device(): lax.all_to_all(partial_rows, 'exp', split_axis=0, concat_axis=0, tiled=True)  15.3 us
    slice x1, local copies, waits for them, and re-layouts, on_device(): w_out = expert_weights[0, :, 1, :]  11.3 us
    all_to_all x1, starting transfers between devices, on_device(): lax.all_to_all(send_rows, 'exp', split_axis=0, concat_axis=0, tiled=True)  6.35 us
    reduce_sum x1, other arithmetic, on_device(): jnp.sum(picked_rows.astype(jnp.float32).reshape(tokens, TOP, model_width)...  5.99 us
  transfers between devices with their start and end apart: 4, of which 4 were waited for; matrix products, arithmetic and copies ran while one was open for 29% of the time, Pallas kernels for 0%

commit v1 on v0

v1 whole, which is shorter than its diff:
```python
import jax
import jax.numpy as jnp
from jax import lax
from jax.sharding import PartitionSpec as P

HEADS = 20
HEAD = 128
TOP = 2


EPSILON = 1e-05


def on_device(
    states, out_grad, doc_keys, doc_values, norm_gain, expert_ids, gate_values, expert_weights
):
    tokens = states.shape[1]
    model_width = states.shape[2]
    key_count = doc_keys.shape[1]
    scale = HEAD ** (-0.5)
    inputs = states[0].astype(jnp.float32)
    inverse = lax.rsqrt(jnp.mean(inputs * inputs, axis=-1, keepdims=True) + EPSILON)
    unit = inputs * inverse
    normed = (unit * norm_gain).astype(jnp.bfloat16)
    upstream = out_grad[0]
    queries = normed.reshape(tokens, HEADS, HEAD)
    key_heads = doc_keys[0].reshape(key_count, HEADS, HEAD)
    value_heads = doc_values[0].reshape(key_count, HEADS, HEAD)
    grad_heads = upstream.reshape(tokens, HEADS, HEAD)
    scores = (
        jnp.einsum("qhd,khd->hqk", queries, key_heads, preferred_element_type=jnp.float32) * scale
    )
    local_peak = jnp.max(scores, axis=-1)
    local_weights = jnp.exp(scores - local_peak[..., None])
    local_total = jnp.sum(local_weights, axis=-1)
    slopes = jnp.einsum("qhd,khd->hqk", grad_heads, value_heads, preferred_element_type=jnp.float32)
    local_inner = jnp.sum(local_weights * slopes, axis=-1)
    stats = lax.all_gather(jnp.stack([local_peak, local_total, local_inner]), "ctx")
    peak = jnp.max(stats[:, 0], axis=0)
    factors = jnp.exp(stats[:, 0] - peak[None])
    total = jnp.sum(stats[:, 1] * factors, axis=0)
    merged = jnp.sum(stats[:, 2] * factors, axis=0)
    delta = merged / total
    probs = jnp.exp(scores - peak[..., None]) / total[..., None]
    score_grad = (probs * (slopes - delta[..., None])).astype(jnp.bfloat16)
    probs_low = probs.astype(jnp.bfloat16)
    values_grad = jnp.einsum(
        "hqk,qhd->khd", probs_low, grad_heads, preferred_element_type=jnp.float32
    )
    keys_grad = (
        jnp.einsum("hqk,qhd->khd", score_grad, queries, preferred_element_type=jnp.float32) * scale
    )
    query_grad = (
        jnp.einsum(
            "hqk,khd->qhd", score_grad, key_heads, preferred_element_type=jnp.float32
        ).reshape(tokens, model_width)
        * scale
    )
    ctx_count = lax.axis_size("ctx")
    expert_count = lax.axis_size("exp")
    capacity = ctx_count * (
        (5 * TOP * tokens + 4 * expert_count * ctx_count - 1) // (4 * expert_count * ctx_count)
    )
    ids = expert_ids[0]
    named = ids[:, :, None] == jnp.arange(expert_count, dtype=jnp.int32)[None, None, :]
    chosen = jnp.any(named, axis=1).astype(jnp.bfloat16)
    gates = jnp.sum(jnp.where(named, gate_values[0][:, :, None], 0.0), axis=1)
    before = jnp.tri(tokens, k=-1, dtype=jnp.bfloat16)
    slot = jnp.dot(before, chosen, preferred_element_type=jnp.float32)
    slot = jnp.where(chosen > 0, slot, -1.0)
    select = slot.T[:, None, :] == jnp.arange(capacity, dtype=jnp.float32)[None, :, None]
    slot_gate = jnp.sum(jnp.where(select, gates.T[:, None, :], 0.0), axis=-1)
    select = select.astype(jnp.bfloat16).reshape(expert_count * capacity, tokens)
    me = lax.axis_index("ctx")
    share = model_width // ctx_count
    own_normed = lax.dynamic_slice_in_dim(normed, me * share, share, 1)
    own_upstream = lax.dynamic_slice_in_dim(upstream, me * share, share, 1)
    send_rows = jnp.dot(select, own_normed, preferred_element_type=jnp.float32)
    send_grads = jnp.dot(select, own_upstream, preferred_element_type=jnp.float32)
    send_grads = send_grads * slot_gate.reshape(-1, 1)
    sends = jnp.stack([send_rows, send_grads]).astype(jnp.bfloat16)
    sends = sends.reshape(2, expert_count, capacity, share)
    got = lax.all_to_all(sends, "exp", split_axis=1, concat_axis=1, tiled=True)
    slot_rows = expert_count * capacity
    got = lax.all_gather(got.reshape(2, slot_rows, share), "ctx", axis=2, tiled=True)
    rows, douts = got[0], got[1]
    w_in = expert_weights[0, :, 0, :]
    w_out = expert_weights[0, :, 1, :]
    pre = jnp.einsum("sd,hd->sh", rows, w_in, preferred_element_type=jnp.float32)
    activ, pull = jax.vjp(jax.nn.gelu, pre)
    activ_low = activ.astype(jnp.bfloat16)
    act_grad = jnp.einsum("sd,hd->sh", douts, w_out, preferred_element_type=jnp.float32)
    pre_grad = pull(act_grad)[0].astype(jnp.bfloat16)
    grad_in = jnp.einsum("sh,sd->hd", pre_grad, rows, preferred_element_type=jnp.float32)
    grad_proj = jnp.einsum("sh,sd->hd", activ_low, douts, preferred_element_type=jnp.float32)
    weights_grad = jnp.stack([grad_in, grad_proj], axis=1).astype(jnp.bfloat16)[None]
    partial_rows = jnp.einsum("sh,hd->sd", pre_grad, w_in, preferred_element_type=jnp.float32)
    partial_rows = lax.psum_scatter(
        partial_rows.astype(jnp.bfloat16), "ctx", scatter_dimension=1, tiled=True
    ).reshape(expert_count, capacity, share)
    returned = lax.all_to_all(partial_rows, "exp", split_axis=0, concat_axis=0, tiled=True)
    moe_part = jnp.einsum(
        "st,sd->td", select, returned.reshape(slot_rows, share), preferred_element_type=jnp.float32
    )
    query_part = lax.psum_scatter(
        query_grad.astype(jnp.bfloat16), "ctx", scatter_dimension=1, tiled=True
    )
    total_grad = (query_part.astype(jnp.float32) + moe_part).astype(jnp.bfloat16)
    total_grad = lax.all_gather(total_grad, "ctx", axis=1, tiled=True).astype(jnp.float32)
    scaled = total_grad * norm_gain
    states_grad = upstream.astype(jnp.float32) + inverse * (
        scaled - unit * jnp.mean(scaled * unit, axis=-1, keepdims=True)
    )
    return (
        states_grad.astype(jnp.bfloat16)[None],
        keys_grad.reshape(key_count, model_width).astype(jnp.bfloat16)[None],
        values_grad.reshape(key_count, model_width).astype(jnp.bfloat16)[None],
        weights_grad,
    )


def solution(mesh):
    return jax.shard_map(
        on_device,
        mesh=mesh,
        in_specs=(
            P("exp", None, None),
            P("exp", None, None),
            P("exp", "ctx", None),
            P("exp", "ctx", None),
            P(),
            P("exp", None, None),
            P("exp", None, None),
            P("exp", "ctx", None, None),
        ),
        out_specs=(
            P("exp", None, None),
            P("exp", "ctx", None),
            P("exp", "ctx", None),
            P("exp", "ctx", None, None),
        ),
        check_vma=False,
    )
```

time: 230 us -> 199 us (0.87)
  blocking collectives: 23.7 us -> 50.5 us
  local copies, waits for them, and re-layouts: 57.8 us -> 38.8 us
  waiting for transfers between devices: 69.9 us -> 54 us
  other arithmetic: 22.1 us -> 9.19 us
  starting transfers between devices: 13.9 us -> 4.91 us
    unnamed x1 -> x5, waiting for transfers between devices: 0.02 us -> 39.6 us
    psum x1 -> x0, waiting for transfers between devices: 29.7 us -> none  [on_device(): lax.psum((query_grad + moe_part).astype(jnp.bfloat16), 'ctx')]
    all_to_all x0 -> x1, blocking collectives: none -> 27.8 us  [on_device(): got = lax.all_to_all(sends, 'exp', split_axis=1, concat_axis=1, tiled=True)]
    all_to_all x2 -> x0, waiting for transfers between devices: 24.8 us -> none  [the longest x1 22 us: on_device(): lax.all_to_all(send_grads, 'exp', split_axis=0, concat_axis=0, tiled=True)]
    all_to_all x1, waiting for transfers between devices: 15.3 us -> 0.01 us  [on_device(): lax.all_to_all(partial_rows, 'exp', split_axis=0, concat_axis=0, tiled=True)]
    all_gather x0 -> x1, waiting for transfers between devices: none -> 14.4 us  [on_device(): lax.all_gather(got.reshape(2, slot_rows, share), 'ctx', axis=2, tiled=True)]
    gather x4 -> x0, local copies, waits for them, and re-layouts: 10.7 us -> none  [the longest x1 3.18 us: on_device(): upstream[source].astype(jnp.float32)]
    all_to_all x2 -> x0, starting transfers between devices: 10.1 us -> none  [the longest x1 6.35 us: on_device(): lax.all_to_all(send_rows, 'exp', split_axis=0, concat_axis=0, tiled=True)]
  transfers between devices with their start and end apart: 4 -> 4, of which waited for: 4 -> 3; matrix products, arithmetic and copies ran while one was open for 29% -> 31% of each run, Pallas kernels for 0% -> 0%
where the time goes in v1:
time: 199 us; the launch traced here: 198 us
  waiting for transfers between devices  54 us (27%)
  blocking collectives  50.5 us (25%)
  local copies, waits for them, and re-layouts  38.8 us (19%)
  matrix products  26.2 us (13%)
  between operations  14 us (7%)
  other arithmetic  9.19 us (5%)
  starting transfers between devices  4.91 us (2%)
    unnamed x5, waiting for transfers between devices  39.6 us
    all_to_all x1, blocking collectives, on_device(): got = lax.all_to_all(sends, 'exp', split_axis=1, concat_axis=1, tiled=True)  27.8 us
    unnamed x39, local copies, waits for them, and re-layouts  24.4 us
    all_gather x1, waiting for transfers between devices, on_device(): lax.all_gather(got.reshape(2, slot_rows, share), 'ctx', axis=2, tiled=True)  14.4 us
    all_gather x1, blocking collectives, on_device(): lax.all_gather(total_grad, 'ctx', axis=1, tiled=True).astype(jnp.float32)  12.7 us
    slice x1, local copies, waits for them, and re-layouts, on_device(): w_out = expert_weights[0, :, 1, :]  11.5 us
    all_gather x1, blocking collectives, on_device(): lax.all_gather(jnp.stack([local_peak, local_total, local_inner]), 'ctx')  10 us
    all_to_all x1, starting transfers between devices, on_device(): lax.all_to_all(partial_rows, 'exp', split_axis=0, concat_axis=0, tiled=True)  4.61 us
  transfers between devices with their start and end apart: 4, of which 3 were waited for; matrix products, arithmetic and copies ran while one was open for 31% of the time, Pallas kernels for 0%

profile of v1, /device:TPU:0, one launch (start us, length us, event | category | flops | bytes accessed | tf_op | source)
XLA Modules:
  0.0 197.7 jit_solution(11736530306077764649)
XLA Ops:
  7.2 0.7 fusion.41
  7.9 0.2 convolution_select_fusion
  8.2 0.7 select_reduce_fusion.1
  8.9 0.1 select_reduce_fusion
  9.1 1.3 fusion.7
  10.4 1.3 bitcast_multiply_fusion
  11.8 0.3 fusion.10
  12.1 0.3 fusion.9
  12.4 0.1 pad_maximum_fusion.1
  12.6 27.8 %all_to_all.10 = bf16[2,8,40,640]{3,2,0,1:T(8,128)(2,1)S(1)} all-to-all(bf16[2,8,40,640]{3,2,0,1:T(8,128)(2,1)S(1)} %copy.114), channel_id=1, replica_groups=mesh['ctx'=4,'exp'=8] {'exp'}, dimensions={1} | all-to-all | bytes 1638400 | tf_op jit(solution)/shard_map/all_to_all | solution.py:83
  40.4 1.0 copy.115
  41.5 0.2 copy-done
  41.7 0.2 copy.102
  41.9 1.1 copy.106
  43.0 1.1 copy.103
  44.1 1.1 copy.107
  45.2 2.0 fusion.49
  47.2 0.5 fusion.13
  47.7 10.0 %all-gather = f32[12,20,128]{2,1,0:T(8,128)S(1)} all-gather(f32[3,20,128]{2,1,0:T(8,128)S(1)} %pad_maximum_fusion.2), channel_id=2, replica_groups=mesh['ctx'=4,'exp'=8] {'ctx'}, dimensions={0}, use_global_device_ids=true | all-gather | bytes 153600 | tf_op jit(solution)/shard_map/all_gather | solution.py:38
  57.8 0.4 multiply_convert_fusion
  58.2 0.8 copy-done.1
  59.0 1.2 fusion.5
  60.2 0.2 reduce-scatter.9.cloned.1.call-start
  60.4 11.5 %fusion.48 = (bf16[1,512,1,2560]{3,2,1,0:T(2,128)(2,1)}, bf16[1,512,1,2560]{3,2,1,0:T(2,128)(2,1)}) fusion(bf16[1,512,2,2560]{3,2,1,0:T(2,128)(2,1)} %param.15), kind=kLoop, calls=%fused_computation.91 | loop fusion | bytes 10485760 | tf_op jit(solution)/shard_map/slice | solution.py:88
  71.9 14.4 %all-gather.3.cloned.1.call-done = bf16[2,320,2560]{2,1,0:T(8,128)(2,1)} async-done(((bf16[2,320,640]{2,1,0:T(8,128)(2,1)}), bf16[2,320,2560]{2,1,0:T(8,128)(2,1)}) %all-gather.3.cloned.1.call-update) | async-done | bytes 3276816 | tf_op jit(solution)/shard_map/all_gather | solution.py:85
  86.4 4.2 %fusion.3 = f32[320,512]{1,0:T(8,128)S(1)} fusion(bf16[2,320,2560]{2,1,0:T(8,128)(2,1)} %all-gather.3.cloned.1.call-done, bf16[1,512,1,2560]{3,2,1,0:T(2,128)(2,1)} %get-tuple-element.29), kind=kOutput, calls=%fused_computation.11 | convolution fusion | flops 838860800 | bytes 7536640 | tf_op jit(solution)/shard_map/sd,hd->sh/dot_general | solution.py:89
  90.6 4.6 %fusion.20 = bf16[320,512]{1,0:T(8,128)(2,1)S(1)} fusion(f32[320,512]{1,0:T(8,128)S(1)} %fusion.3, bf16[1,512,1,2560]{3,2,1,0:T(2,128)(2,1)} %get-tuple-element.28, bf16[2,320,2560]{2,1,0:T(8,128)(2,1)} %all-gather.3.cloned.1.call-done), kind=kOutput, calls=%fused_computation.49 | convolution fusion | flops 842137600 | bytes 7864320 | tf_op jit(solution)/shard_map/sd,hd->sh/dot_general | solution.py:92
  95.2 0.7 copy-done.11
  95.9 2.2 %convolution_convert_fusion.2 = bf16[320,2560]{1,0:T(8,128)(2,1)} fusion(bf16[320,512]{1,0:T(8,128)(2,1)S(1)} %fusion.20, bf16[1,512,1,2560]{3,2,1,0:T(2,128)(2,1)S(1)} %bitcast.126), kind=kOutput, calls=%fused_computation.5 | convolution fusion | flops 839680000 | bytes 4587520 | tf_op jit(solution)/shard_map/sh,hd->sd/dot_general | solution.py:97
  98.1 3.9 %copy.135 = bf16[320,2560]{0,1:T(8,128)(2,1)} copy(bf16[320,2560]{1,0:T(8,128)(2,1)} %convolution_convert_fusion.2) | data formatting | bytes 3276800
  102.0 2.6 %fusion.8 = bf16[128,20,128]{2,0,1:T(8,128)(2,1)} fusion(bf16[20,128,128]{1,2,0:T(8,128)(2,1)} %copy-done.1, f32[128,20,128]{0,2,1:T(8,128)S(1)} %bitcast.121, f32[20,128]{1,0:T(8,128)S(1)} %bitcast.140, f32[128]{0:T(128)S(1)} %add_rsqrt_fusion), kind=kOutput, calls=%fused_computation.31 | convolution fusion | flops 85524480 | bytes 2632192 | tf_op jit(solution)/shard_map/hqk,qhd->khd/dot_general | solution.py:51
  104.6 1.5 copy.120
  106.0 1.1 copy.122
  107.1 0.6 convolution_convert_fusion.3
  107.7 1.1 copy.123
  108.8 6.1 %reduce-scatter.7.cloned.1.call-done = bf16[640,128]{1,0:T(8,128)(2,1)} async-done(((bf16[2560,128]{1,0:T(8,128)(2,1)}), bf16[640,128]{1,0:T(8,128)(2,1)}) %reduce-scatter.7.cloned.1.call-update) | async-done | bytes 163856
  114.9 1.1 copy.134
  116.0 3.2 %fusion.1 = bf16[1,512,1,2560]{3,1,2,0:T(8,128)(2,1)S(1)} fusion(bf16[2,320,2560]{2,1,0:T(8,128)(2,1)} %all-gather.3.cloned.1.call-done, f32[320,512]{1,0:T(8,128)} %copy-done.12), kind=kOutput, calls=%fused_computation.4 | convolution fusion | flops 841646080 | bytes 4915200 | tf_op jit(solution)/shard_map/sh,sd->hd/dot_general | solution.py:95
  119.2 33.5 %reduce-scatter.9.cloned.1.call-done = bf16[640,320]{1,0:T(8,128)(2,1)} async-done(((bf16[2560,320]{1,0:T(8,128)(2,1)}), bf16[640,320]{1,0:T(8,128)(2,1)}) %reduce-scatter.9.cloned.1.call-update) | async-done | bytes 409616
  152.7 2.0 copy.136
  154.7 4.6 %all-to-all-start.1 = ((bf16[8,40,640]{2,1,0:T(8,128)(2,1)}), bf16[8,40,640]{2,1,0:T(8,128)(2,1)}, u32[]{:S(2)}, u32[]{:S(2)}) async-start(bf16[8,40,640]{2,1,0:T(8,128)(2,1)} %bitcast.133), calls=%async_computation.1 | async-start | bytes 819200 | tf_op jit(solution)/shard_map/all_to_all | solution.py:101
  159.3 3.1 %fusion = bf16[1,512,1,2560]{3,1,2,0:T(8,128)(2,1)S(1)} fusion(bf16[320,512]{1,0:T(8,128)(2,1)} %copy-done.11, bf16[2,320,2560]{2,1,0:T(8,128)(2,1)} %all-gather.3.cloned.1.call-done), kind=kOutput, calls=%fused_computation.3 | convolution fusion | flops 840171520 | bytes 4587520 | tf_op jit(solution)/shard_map/sh,sd->hd/dot_general | solution.py:94
  162.4 2.8 %pad_maximum_fusion = bf16[1,512,2,2560]{3,1,2,0:T(8,128)(2,1)} fusion(bf16[1,512,1,2560]{3,1,2,0:T(8,128)(2,1)S(1)} %fusion.1, bf16[1,512,1,2560]{3,1,2,0:T(8,128)(2,1)S(1)} %fusion), kind=kLoop, calls=%fused_computation | loop fusion | flops 2621440 | bytes 10485760 | tf_op jit(solution)/shard_map/stack | solution.py:96
  165.1 10.2 %copy.124 = bf16[1,512,2,2560]{3,2,1,0:T(2,128)(2,1)} copy(bf16[1,512,2,2560]{3,1,2,0:T(8,128)(2,1)} %pad_maximum_fusion) | data formatting | bytes 10485760
  175.4 1.4 fusion.12
  176.8 12.7 %all_gather.15 = bf16[128,2560]{1,0:T(8,128)(2,1)S(1)} all-gather(bf16[128,640]{1,0:T(8,128)(2,1)S(1)} %fusion.12), channel_id=1, replica_groups=mesh['ctx'=4,'exp'=8] {'ctx'}, dimensions={1}, use_global_device_ids=true | all-gather | bytes 819200 | tf_op jit(solution)/shard_map/all_gather | solution.py:109
  189.4 0.4 multiply_reduce_fusion
  189.9 1.3 fusion.21
  (45 shorter events, 0.5 us)
Async XLA Ops:
  7.2 79.2 %all-gather.3.cloned.1.call-start = ((), (), s32[]{:S(2)}) async-start(), calls=%async_computation.4 | async-start | bytes 4096000 | tf_op jit(solution)/shard_map/all_gather | solution.py:85
  9.1 2.7 %copy-start.10 = (f32[2560]{0:T(1024)S(1)}, f32[2560]{0:T(1024)}, u32[]{:S(2)}) copy-start(f32[2560]{0:T(1024)} %param.12) | copy-start | bytes 30724
  10.4 1.7 copy-start.3
  40.4 1.3 copy-start
  41.4 1.6 copy-start.8
  41.4 73.5 %reduce-scatter.7.cloned.1.call-start = ((), (), s32[]{:S(2)}) async-start(), calls=%async_computation.5 | async-start | bytes 819200
  43.0 1.1 copy-start.9
  45.2 2.0 copy-start.5
  45.2 2.0 %copy-start.7 = (bf16[1,128,2560]{1,2,0:T(8,128)(2,1)S(1)}, bf16[1,128,2560]{1,2,0:T(8,128)(2,1)}, u32[]{:S(2)}) copy-start(bf16[1,128,2560]{1,2,0:T(8,128)(2,1)} %copy.107) | copy-start | bytes 1966084
  57.8 1.2 copy-start.2
  58.2 0.8 copy-start.1
  60.2 92.5 %reduce-scatter.9.cloned.1.call-start = ((), (), s32[]{:S(2)}) async-start(), calls=%async_computation.6 | async-start | bytes 2457600
  86.4 9.5 %slice-start = ((s8[5242880]{0:T(1024)(128)(4,1)}), s8[4194304]{0:T(1024)(128)(4,1)S(1)}, s32[]{:S(2)}) async-start(s8[5242880]{0:T(1024)(128)(4,1)} %bitcast.125), calls=%async_computation.7 | async-start | bytes 8388608
  90.5 4.6 %copy-start.12 = (f32[320,512]{1,0:T(8,128)}, f32[320,512]{1,0:T(8,128)S(1)}, u32[]{:S(2)}) copy-start(f32[320,512]{1,0:T(8,128)S(1)} %fusion.3) | copy-start | bytes 1966084
  90.5 5.3 %slice-start.1 = ((s8[5242880]{0:T(1024)(128)(4,1)}), s8[1048576]{0:T(1024)(128)(4,1)S(1)}, s32[]{:S(2)}) async-start(s8[5242880]{0:T(1024)(128)(4,1)} %bitcast.125), calls=%async_computation.8 | async-start | bytes 2097152
  95.2 0.7 copy-start.11
  104.6 2.6 %copy-start.6 = (bf16[1,128,2560]{1,2,0:T(8,128)(2,1)S(1)}, bf16[1,128,2560]{1,2,0:T(8,128)(2,1)}, u32[]{:S(2)}) copy-start(bf16[1,128,2560]{1,2,0:T(8,128)(2,1)} %copy.106) | copy-start | bytes 1966084
  154.7 20.7 %all-to-all-start.1 = ((bf16[8,40,640]{2,1,0:T(8,128)(2,1)}), bf16[8,40,640]{2,1,0:T(8,128)(2,1)}, u32[]{:S(2)}, u32[]{:S(2)}) async-start(bf16[8,40,640]{2,1,0:T(8,128)(2,1)} %bitcast.133), calls=%async_computation.1 | async-start | bytes 819200 | tf_op jit(solution)/shard_map/all_to_all | solution.py:101
  175.4 14.5 %copy-start.4 = (bf16[1,128,2560]{2,1,0:T(8,128)(2,1)S(1)}, bf16[1,128,2560]{2,1,0:T(8,128)(2,1)}, u32[]{:S(2)}) copy-start(bf16[1,128,2560]{2,1,0:T(8,128)(2,1)} %param.9) | copy-start | bytes 1966084
Sparse Core Ops, SparseCore 0:
  41.5 44.7 all-gather.2
  89.2 25.6 reduce-scatter.6
  118.6 34.0 reduce-scatter.8

commit v2 on v1

v2 whole, which is shorter than its diff:
```python
import functools
import jax
import jax.numpy as jnp
from jax import lax
from jax.experimental import pallas as pl
from jax.experimental.pallas import tpu as pltpu
from jax.sharding import PartitionSpec as P

HEADS = 20
HEAD = 128
TOP = 2


EPSILON = 1e-05
MESH = pl.DeviceIdType.MESH
F32 = jnp.float32
BF16 = jnp.bfloat16
VMEM_LIMIT = 60 * 1024 * 1024


def dot(a, b, ca, cb):
    return lax.dot_general(a, b, (((ca,), (cb,)), ((), ())), preferred_element_type=F32)


def head_cols(h):
    return pl.ds(pl.multiple_of(h * HEAD, HEAD), HEAD)


def front_kernel(experts, capacity, states, upstream, keys, values, gain, ids, gates, normed, sends, select, stats):
    tokens = states.shape[0]
    inputs = states[...].astype(F32)
    inverse = lax.rsqrt(jnp.mean(inputs * inputs, axis=-1, keepdims=True) + EPSILON)
    normed[...] = (inputs * inverse * gain[...]).astype(BF16)
    expert = lax.broadcasted_iota(jnp.int32, (experts, tokens), 0)
    first, second = ids[0:1, :] == expert, ids[1:2, :] == expert
    chosen = jnp.where(first | second, 1.0, 0.0)
    gate = jnp.where(first, gates[0:1, :], jnp.where(second, gates[1:2, :], 0.0))
    row = lax.broadcasted_iota(jnp.int32, (tokens, tokens), 0)
    col = lax.broadcasted_iota(jnp.int32, (tokens, tokens), 1)
    before = jnp.where(row < col, 1.0, 0.0).astype(BF16)
    slot = dot(chosen.astype(BF16), before, 1, 0)
    slot = jnp.where(chosen > 0.5, slot, -1.0)
    number = lax.broadcasted_iota(jnp.int32, (capacity, tokens), 0).astype(F32)
    for e in range(experts):
        picked = jnp.where(slot[e : e + 1, :] == number, 1.0, 0.0)
        slot_gate = jnp.sum(picked * gate[e : e + 1, :], axis=1, keepdims=True)
        picked = picked.astype(BF16)
        select[e] = picked
        sends[0, e] = dot(picked, normed[...], 1, 0).astype(BF16)
        sends[1, e] = (dot(picked, upstream[...], 1, 0) * slot_gate).astype(BF16)

    def one(h, carry):
        cols = head_cols(h)
        scores = dot(keys[:, cols], normed[:, cols], 1, 1) * HEAD ** (-0.5)
        peak = jnp.max(scores, axis=0, keepdims=True)
        weights = jnp.exp(scores - peak)
        slopes = dot(values[:, cols], upstream[:, cols], 1, 1)
        stats[0, pl.ds(h, 1), :] = peak
        stats[1, pl.ds(h, 1), :] = jnp.sum(weights, axis=0, keepdims=True)
        stats[2, pl.ds(h, 1), :] = jnp.sum(weights * slopes, axis=0, keepdims=True)
        return carry

    lax.fori_loop(0, HEADS, one, 0, unroll=4)


def entry_barrier(ctx_count, experts, c, e):
    barrier = pltpu.get_barrier_semaphore()
    for d in range(1, ctx_count):
        pl.semaphore_signal(barrier, inc=1, device_id={"ctx": lax.rem(c + d, ctx_count), "exp": e}, device_id_type=MESH)
    for d in range(1, experts):
        pl.semaphore_signal(barrier, inc=1, device_id={"ctx": c, "exp": lax.rem(e + d, experts)}, device_id_type=MESH)
    pl.semaphore_wait(barrier, ctx_count + experts - 2)


def dispatch_kernel(
    ctx_count, experts, normed, upstream, keys, values, sends, stats,
    got, keys_grad, values_grad, query_grad,
    stats_all, merged, direct_sem, forward_sem, got_sem, stats_send, stats_got,
):
    c, e = lax.axis_index("ctx"), lax.axis_index("exp")
    entry_barrier(ctx_count, experts, c, e)

    def stats_copy(d):
        peer = lax.rem(c + d, ctx_count)
        return pltpu.make_async_remote_copy(
            src_ref=stats, dst_ref=stats_all.at[ctx_count - 1 - d],
            send_sem=stats_send.at[d - 1], recv_sem=stats_got.at[ctx_count - 1 - d],
            device_id={"ctx": peer, "exp": e}, device_id_type=MESH,
        )

    def direct_copy(t, d):
        to = lax.rem(e + d, experts)
        return pltpu.make_async_remote_copy(
            src_ref=sends.at[t, to], dst_ref=got.at[t, e],
            send_sem=direct_sem.at[t, d], recv_sem=got_sem.at[t, e],
            device_id={"ctx": c, "exp": to}, device_id_type=MESH,
        )

    def forward_copy(t, s, d):
        return pltpu.make_async_remote_copy(
            src_ref=got.at[t, s], dst_ref=got.at[t, s],
            send_sem=forward_sem.at[t, s, d - 1], recv_sem=got_sem.at[t, s],
            device_id={"ctx": lax.rem(c + d, ctx_count), "exp": e}, device_id_type=MESH,
        )

    def goes(d):
        return (lax.rem(e, ctx_count) == c) | (lax.rem(e + d, experts) // 2 == e // 2)

    for d in range(1, ctx_count):
        stats_copy(d).start()
    for t in range(2):
        for d in range(1, experts):
            @pl.when(goes(d))
            def _():
                direct_copy(t, d).start()
    for t in range(2):
        got[t, e] = sends[t, e]
    for d in range(1, ctx_count):
        stats_copy(d).wait()
    peak = stats[0]
    for d in range(ctx_count - 1):
        peak = jnp.maximum(peak, stats_all[d, 0])
    factor = jnp.exp(stats[0] - peak)
    total, inner = stats[1] * factor, stats[2] * factor
    for d in range(ctx_count - 1):
        factor = jnp.exp(stats_all[d, 0] - peak)
        total = total + stats_all[d, 1] * factor
        inner = inner + stats_all[d, 2] * factor
    merged[0] = peak
    merged[1] = total
    merged[2] = inner / total

    def one(h, carry):
        cols = head_cols(h)
        k, q, g = keys[:, cols], normed[:, cols], upstream[:, cols]
        scores = dot(k, q, 1, 1) * HEAD ** (-0.5)
        probs = jnp.exp(scores - merged[0, pl.ds(h, 1), :]) / merged[1, pl.ds(h, 1), :]
        slopes = dot(values[:, cols], g, 1, 1)
        score_grad = (probs * (slopes - merged[2, pl.ds(h, 1), :])).astype(BF16)
        values_grad[:, cols] = dot(probs.astype(BF16), g, 1, 0).astype(BF16)
        keys_grad[:, cols] = (dot(score_grad, q, 1, 0) * HEAD ** (-0.5)).astype(BF16)
        query_grad[:, cols] = (dot(score_grad, k, 0, 0) * HEAD ** (-0.5)).astype(BF16)
        return carry

    lax.fori_loop(0, HEADS, one, 0)

    def got_copy(t, s):
        return pltpu.make_async_remote_copy(
            src_ref=got.at[t, s], dst_ref=got.at[t, s],
            send_sem=direct_sem.at[t, 0], recv_sem=got_sem.at[t, s],
            device_id={"ctx": c, "exp": lax.rem(e + 1, experts)}, device_id_type=MESH,
        )

    for t in range(2):
        for s in range(experts):
            @pl.when((s % ctx_count == c) & (s // 2 != e // 2))
            def _():
                got_copy(t, s).wait_recv()
                for d in range(1, ctx_count):
                    forward_copy(t, s, d).start()
    for t in range(2):
        for s in range(experts):
            @pl.when((s != e) & ((s % ctx_count != c) | (s // 2 == e // 2)))
            def _():
                got_copy(t, s).wait_recv()
    for t in range(2):
        for s in range(experts):
            @pl.when((s % ctx_count == c) & (s // 2 != e // 2))
            def _():
                for d in range(1, ctx_count):
                    forward_copy(t, s, d).wait_send()
        for d in range(1, experts):
            @pl.when(goes(d))
            def _():
                direct_copy(t, d).wait_send()


def return_kernel(
    ctx_count, experts, width, partial, query_grad, select, total,
    parts, query_parts, reduced, returned, mine, finals,
    part_send, part_got, query_send, query_got, back_send, back_got, final_send, final_got,
):
    c, e = lax.axis_index("ctx"), lax.axis_index("exp")
    tiles = partial.shape[-1] // HEAD
    entry_barrier(ctx_count, experts, c, e)

    def share(owner):
        return pl.ds(pl.multiple_of((owner * tiles // ctx_count) * HEAD, HEAD), width)

    def to_ctx(src, dst, send, recv, d):
        return pltpu.make_async_remote_copy(
            src_ref=src, dst_ref=dst.at[ctx_count - 1 - d], send_sem=send, recv_sem=recv,
            device_id={"ctx": lax.rem(c + d, ctx_count), "exp": e}, device_id_type=MESH,
        )

    def part_copy(d, o):
        peer = lax.rem(c + d, ctx_count)
        s = lax.rem(e + o, experts)
        return pltpu.make_async_remote_copy(
            src_ref=partial.at[s, :, share(peer)], dst_ref=parts.at[ctx_count - 1 - d, s],
            send_sem=part_send.at[d - 1, o], recv_sem=part_got.at[ctx_count - 1 - d, o],
            device_id={"ctx": peer, "exp": e}, device_id_type=MESH,
        )

    def query_copy(d):
        peer = lax.rem(c + d, ctx_count)
        return to_ctx(query_grad.at[:, share(peer)], query_parts, query_send.at[d - 1], query_got.at[ctx_count - 1 - d], d)

    def back_copy(o):
        s = lax.rem(e + o, experts)
        return pltpu.make_async_remote_copy(
            src_ref=reduced.at[s], dst_ref=returned.at[e],
            send_sem=back_send.at[o], recv_sem=back_got.at[experts - o],
            device_id={"ctx": c, "exp": s}, device_id_type=MESH,
        )

    def final_copy(d):
        return to_ctx(mine, finals, final_send.at[d - 1], final_got.at[ctx_count - 1 - d], d)

    order = sorted(range(experts), key=lambda o: (o == 0, abs(o - experts // 2)))
    for o in order:
        for d in range(1, ctx_count):
            part_copy(d, o).start()
    for d in range(1, ctx_count):
        query_copy(d).start()
    for o in order:
        for d in range(1, ctx_count):
            part_copy(d, o).wait()
        s = lax.rem(e + o, experts)
        summed = partial[s, :, share(c)].astype(F32)
        for d in range(ctx_count - 1):
            summed = summed + parts[d, s].astype(F32)
        if o == 0:
            returned[s] = summed.astype(BF16)
        else:
            reduced[s] = summed.astype(BF16)
            back_copy(o).start()
    summed = query_grad[:, share(c)].astype(F32)
    for d in range(1, ctx_count):
        query_copy(d).wait()
    for d in range(ctx_count - 1):
        summed = summed + query_parts[d].astype(F32)
    for o in range(1, experts):
        back_copy(o).wait()
    for s in range(experts):
        summed = summed + dot(select[s], returned[s], 0, 0)
    mine[...] = summed.astype(BF16)
    for d in range(1, ctx_count):
        final_copy(d).start()
    total[:, share(c)] = mine[...]
    for d in range(1, ctx_count):
        final_copy(d).wait()
    for d in range(1, ctx_count):
        owner = lax.rem(c + d, ctx_count)
        total[:, share(owner)] = finals[d - 1]


def on_device(
    states, out_grad, doc_keys, doc_values, norm_gain, expert_ids, gate_values, expert_weights
):
    tokens = states.shape[1]
    model_width = states.shape[2]
    key_count = doc_keys.shape[1]
    ctx_count = lax.axis_size("ctx")
    expert_count = lax.axis_size("exp")
    capacity = ctx_count * (
        (5 * TOP * tokens + 4 * expert_count * ctx_count - 1) // (4 * expert_count * ctx_count)
    )
    upstream = out_grad[0]
    vmem = pl.BlockSpec(memory_space=pltpu.VMEM)
    shape = jax.ShapeDtypeStruct
    dma = pltpu.SemaphoreType.DMA
    normed, sends, select, stats = pl.pallas_call(
        functools.partial(front_kernel, expert_count, capacity),
        out_shape=(
            shape((tokens, model_width), BF16),
            shape((2, expert_count, capacity, model_width), BF16),
            shape((expert_count, capacity, tokens), BF16),
            shape((3, HEADS, tokens), F32),
        ),
        in_specs=[vmem] * 7,
        out_specs=(vmem,) * 4,
        compiler_params=pltpu.CompilerParams(vmem_limit_bytes=VMEM_LIMIT),
    )(states[0], upstream, doc_keys[0], doc_values[0], norm_gain[None], expert_ids[0].T, gate_values[0].T)
    got, keys_grad, values_grad, query_grad = pl.pallas_call(
        functools.partial(dispatch_kernel, ctx_count, expert_count),
        out_shape=(
            shape((2, expert_count, capacity, model_width), BF16),
            shape((key_count, model_width), BF16),
            shape((key_count, model_width), BF16),
            shape((tokens, model_width), BF16),
        ),
        in_specs=[vmem] * 6,
        out_specs=(vmem,) * 4,
        scratch_shapes=[
            pltpu.VMEM((ctx_count - 1, 3, HEADS, tokens), F32),
            pltpu.VMEM((3, HEADS, tokens), F32),
            dma((2, expert_count)),
            dma((2, expert_count, ctx_count - 1)),
            dma((2, expert_count)),
            dma((ctx_count - 1,)),
            dma((ctx_count - 1,)),
        ],
        compiler_params=pltpu.CompilerParams(
            vmem_limit_bytes=VMEM_LIMIT, collective_id=0, has_side_effects=True
        ),
    )(normed, upstream, doc_keys[0], doc_values[0], sends, stats)
    slot_rows = expert_count * capacity
    rows = got[0].reshape(slot_rows, model_width)
    douts = got[1].reshape(slot_rows, model_width)
    w_in = expert_weights[0, :, 0, :]
    w_out = expert_weights[0, :, 1, :]
    pre = jnp.einsum("sd,hd->sh", rows, w_in, preferred_element_type=jnp.float32)
    activ, pull = jax.vjp(jax.nn.gelu, pre)
    activ_low = activ.astype(jnp.bfloat16)
    act_grad = jnp.einsum("sd,hd->sh", douts, w_out, preferred_element_type=jnp.float32)
    pre_grad = pull(act_grad)[0].astype(jnp.bfloat16)
    grad_in = jnp.einsum("sh,sd->hd", pre_grad, rows, preferred_element_type=jnp.float32)
    grad_proj = jnp.einsum("sh,sd->hd", activ_low, douts, preferred_element_type=jnp.float32)
    weights_grad = jnp.stack([grad_in, grad_proj], axis=1).astype(jnp.bfloat16)[None]
    partial_rows = jnp.einsum("sh,hd->sd", pre_grad, w_in, preferred_element_type=jnp.float32)
    tiles = model_width // HEAD
    width = HEAD * max(
        (c + 1) * tiles // ctx_count + ((c + 1) * tiles % ctx_count > 0) - c * tiles // ctx_count
        for c in range(ctx_count)
    )
    total_grad = pl.pallas_call(
        functools.partial(return_kernel, ctx_count, expert_count, width),
        out_shape=shape((tokens, model_width), BF16),
        in_specs=[vmem] * 3,
        out_specs=vmem,
        scratch_shapes=[
            pltpu.VMEM((ctx_count - 1, expert_count, capacity, width), BF16),
            pltpu.VMEM((ctx_count - 1, tokens, width), BF16),
            pltpu.VMEM((expert_count, capacity, width), BF16),
            pltpu.VMEM((expert_count, capacity, width), BF16),
            pltpu.VMEM((tokens, width), BF16),
            pltpu.VMEM((ctx_count - 1, tokens, width), BF16),
            dma((ctx_count - 1, expert_count)),
            dma((ctx_count - 1, expert_count)),
            dma((ctx_count - 1,)),
            dma((ctx_count - 1,)),
            dma((expert_count,)),
            dma((expert_count,)),
            dma((ctx_count - 1,)),
            dma((ctx_count - 1,)),
        ],
        compiler_params=pltpu.CompilerParams(
            vmem_limit_bytes=VMEM_LIMIT, collective_id=1, has_side_effects=True
        ),
    )(partial_rows.astype(BF16).reshape(expert_count, capacity, model_width), query_grad, select)
    total_grad = total_grad.astype(F32)
    inputs = states[0].astype(F32)
    inverse = lax.rsqrt(jnp.mean(inputs * inputs, axis=-1, keepdims=True) + EPSILON)
    unit = inputs * inverse
    scaled = total_grad * norm_gain
    states_grad = upstream.astype(jnp.float32) + inverse * (
        scaled - unit * jnp.mean(scaled * unit, axis=-1, keepdims=True)
    )
    return (
        states_grad.astype(jnp.bfloat16)[None],
        keys_grad[None],
        values_grad[None],
        weights_grad,
    )


def solution(mesh):
    return jax.shard_map(
        on_device,
        mesh=mesh,
        in_specs=(
            P("exp", None, None),
            P("exp", None, None),
            P("exp", "ctx", None),
            P("exp", "ctx", None),
            P(),
            P("exp", None, None),
            P("exp", None, None),
            P("exp", "ctx", None, None),
        ),
        out_specs=(
            P("exp", None, None),
            P("exp", "ctx", None),
            P("exp", "ctx", None),
            P("exp", "ctx", None, None),
        ),
        check_vma=False,
    )
```

time: 199 us -> 150 us (0.75)
  Pallas kernels: 0 us -> 111 us
  waiting for transfers between devices: 54 us -> 0 us
  blocking collectives: 50.5 us -> 0 us
  matrix products: 26.2 us -> 7.74 us
  local copies, waits for them, and re-layouts: 38.8 us -> 24.9 us
  between operations: 14 us -> 0.79 us
  starting transfers between devices: 4.91 us -> 0 us
  other arithmetic: 9.19 us -> 5.89 us
    pallas_call x0 -> x3, Pallas kernels: none -> 111 us  [the longest x1 59.2 us: on_device(): pl.pallas_call(functools.partial(dispatch_kernel, ctx_count, expert_count...]
    unnamed x5 -> x0, waiting for transfers between devices: 39.6 us -> none
    all_to_all x1 -> x0, blocking collectives: 27.8 us -> none  [on_device(): got = lax.all_to_all(sends, 'exp', split_axis=1, concat_axis=1, tiled=True)]
    all_gather x2 -> x0, blocking collectives: 22.7 us -> none  [the longest x1 12.7 us: on_device(): lax.all_gather(total_grad, 'ctx', axis=1, tiled=True).astype(jnp.float32)]
    all_gather x1 -> x0, waiting for transfers between devices: 14.4 us -> none  [on_device(): lax.all_gather(got.reshape(2, slot_rows, share), 'ctx', axis=2, tiled=True)]
    unnamed x39 -> x25, local copies, waits for them, and re-layouts: 24.4 us -> 13.7 us
    dot_general x9 -> x0, matrix products: 8.91 us -> none  [the longest x1 2.57 us: on_device(): jnp.einsum('hqk,qhd->khd', score_grad, queries, preferred_element_type=jn...]
    all_to_all x1 -> x0, starting transfers between devices: 4.61 us -> none  [on_device(): lax.all_to_all(partial_rows, 'exp', split_axis=0, concat_axis=0, tiled=True)]
  transfers between devices with their start and end apart: 4 -> 0, of which waited for: 3 -> 0; matrix products, arithmetic and copies ran while one was open for 31% -> 0% of each run, Pallas kernels for 0% -> 0%
where the time goes in v2:
time: 150 us
  Pallas kernels  111 us (74%)
  local copies, waits for them, and re-layouts  24.9 us (17%)
  matrix products  7.74 us (5%)
  other arithmetic  5.89 us (4%)
    pallas_call x1, Pallas kernels, on_device(): pl.pallas_call(functools.partial(dispatch_kernel, ctx_count, expert_count...  59.2 us
    pallas_call x1, Pallas kernels, on_device(): pl.pallas_call(functools.partial(return_kernel, ctx_count, expert_count,...  44.6 us
    unnamed x25, local copies, waits for them, and re-layouts  13.7 us
    slice x1, local copies, waits for them, and re-layouts, on_device(): w_out = expert_weights[0, :, 1, :]  7.6 us
    pallas_call x1, Pallas kernels, on_device(): pl.pallas_call(functools.partial(front_kernel, expert_count, capacity), o...  6.87 us

profile of v2, /device:TPU:0, one launch (start us, length us, event | category | flops | bytes accessed | tf_op | source)
XLA Modules:
  0.0 150.0 jit_solution(3631831442696365879)
XLA Ops:
  0.6 1.3 broadcast_in_dim.16.gain
  1.9 6.9 %shard_map.111 = (bf16[128,2560]{1,0:T(8,128)(2,1)}, bf16[2,8,40,2560]{3,2,1,0:T(8,128)(2,1)}, bf16[8,40,128]{2,1,0:T(8,128)(2,1)}, f32[3,20,128]{2,1,0:T(8,128)}) custom-call(bf16[128,2560]{1,0:T(8,128)(2,1)} %bitcast.40, bf16[128,2560]{1,0:T(8,128)(2,1)} %bitcast.41, bf16[128,2560]{1,0:T(8,128)(2,1)} %bitcast.43, bf16[128,2560]{1,0:T(8,128)(2,1)} %bitcast.45, ...), custom_call_target="tpu_custom_call" | custom-call | tf_op jit(solution)/shard_map/pallas_call | solution.py:273
  8.8 59.2 %shard_map.112 = (bf16[2,8,40,2560]{3,2,1,0:T(8,128)(2,1)}, bf16[128,2560]{1,0:T(8,128)(2,1)}, bf16[128,2560]{1,0:T(8,128)(2,1)}, bf16[128,2560]{1,0:T(8,128)(2,1)}) custom-call(bf16[128,2560]{1,0:T(8,128)(2,1)} %get-tuple-element.12.normed, bf16[128,2560]{1,0:T(8,128)(2,1)} %bitcast.42, bf16[128,2560]{1,0:T(8,128)(2,1)} %bitcast.44, ...), custom_call_target="tpu_custom_call" | custom-call | tf_op jit(solution)/shard_map/pallas_call | solution.py:285
  68.0 0.0 copy-start
  68.0 2.3 %fusion.29 = (bf16[1,8,40,2560]{3,2,1,0:T(8,128)(2,1)S(1)}, bf16[1,8,40,2560]{3,2,1,0:T(8,128)(2,1)S(1)}) fusion(bf16[2,8,40,2560]{3,2,1,0:T(8,128)(2,1)} %get-tuple-element.15), kind=kLoop, calls=%fused_computation.43 | loop fusion | bytes 6553600 | tf_op jit(solution)/shard_map/slice | solution.py:310
  70.3 1.2 copy-done
  71.5 7.6 %fusion.28 = (bf16[1,512,1,2560]{3,2,1,0:T(2,128)(2,1)S(1)}, bf16[1,512,1,2560]{3,2,1,0:T(2,128)(2,1)S(1)}) fusion(bf16[1,512,2,2560]{3,2,1,0:T(2,128)(2,1)S(1)} %copy-done), kind=kLoop, calls=%fused_computation.42 | loop fusion | bytes 10485760 | tf_op jit(solution)/shard_map/slice | solution.py:312
  79.1 1.1 fusion.11
  80.1 0.0 copy-start.7
  80.2 1.3 fusion.18
  81.5 0.0 copy-done.7
  81.5 0.0 copy-start.9
  81.5 2.2 %convolution_convert_fusion.2 = bf16[320,2560]{1,0:T(8,128)(2,1)} fusion(bf16[320,512]{1,0:T(8,128)(2,1)S(1)} %fusion.18, bf16[1,512,1,2560]{3,2,1,0:T(2,128)(2,1)S(1)} %get-tuple-element.29), kind=kOutput, calls=%fused_computation.5 | convolution fusion | flops 839680000 | bytes 4587520 | tf_op jit(solution)/shard_map/sh,hd->sd/dot_general | solution.py:321
  83.7 0.0 copy-done.9
  83.7 0.0 copy-start.1
  83.7 0.0 copy-start.6
  83.7 44.6 %shard_map.113 = bf16[128,2560]{1,0:T(8,128)(2,1)} custom-call(bf16[8,40,2560]{2,1,0:T(8,128)(2,1)} %bitcast.51, bf16[128,2560]{1,0:T(8,128)(2,1)} %get-tuple-element.16.query_grad, bf16[8,40,128]{2,1,0:T(8,128)(2,1)} %get-tuple-element.17.select), custom_call_target="tpu_custom_call" | custom-call | tf_op jit(solution)/shard_map/pallas_call | solution.py:327
  128.4 0.0 copy-done.1
  128.4 0.0 copy-start.2
  128.4 0.0 copy-start.3
  128.4 0.2 fusion.10
  128.6 0.0 copy-done.6
  128.6 1.6 %fusion.5 = f32[128]{0:T(128)S(1)} fusion(bf16[128,2560]{1,0:T(8,128)(2,1)} %shard_map.113, f32[2560]{0:T(1024)S(1)} %copy-done.6, f32[128]{0:T(128)S(1)} %add_rsqrt_fusion, bf16[1,128,2560]{2,1,0:T(8,128)(2,1)S(1)} %copy-done.1), kind=kLoop, calls=%fused_computation.13 | loop fusion | flops 1965952 | bytes 1321984 | tf_op jit(solution)/shard_map/reduce_sum | solution.py:358
  130.2 0.0 copy-start.8
  130.3 0.0 copy-done.2
  130.3 0.0 copy-done.3
  130.3 1.3 fusion.19
  131.6 0.0 copy-done.8
  131.6 0.0 copy-start.10
  131.6 1.6 %fusion.1 = bf16[1,512,1,2560]{3,1,2,0:T(8,128)(2,1)S(1)} fusion(bf16[320,2560]{1,0:T(8,128)(2,1)S(1)} %bitcast.50, f32[320,512]{1,0:T(8,128)S(1)} %copy-done.8), kind=kOutput, calls=%fused_computation.4 | convolution fusion | flops 841646080 | bytes 4915200 | tf_op jit(solution)/shard_map/sh,sd->hd/dot_general | solution.py:319
  133.2 0.0 copy-done.10
  133.2 1.5 %fusion = bf16[1,512,1,2560]{3,1,2,0:T(8,128)(2,1)S(1)} fusion(bf16[320,512]{1,0:T(8,128)(2,1)S(1)} %copy-done.10, bf16[320,2560]{1,0:T(8,128)(2,1)S(1)} %bitcast.48), kind=kOutput, calls=%fused_computation.3 | convolution fusion | flops 840171520 | bytes 4587520 | tf_op jit(solution)/shard_map/sh,sd->hd/dot_general | solution.py:318
  134.8 2.7 %pad_maximum_fusion = bf16[1,512,2,2560]{3,1,2,0:T(8,128)(2,1)} fusion(bf16[1,512,1,2560]{3,1,2,0:T(8,128)(2,1)S(1)} %fusion.1, bf16[1,512,1,2560]{3,1,2,0:T(8,128)(2,1)S(1)} %fusion), kind=kLoop, calls=%fused_computation | loop fusion | flops 2621440 | bytes 10485760 | tf_op jit(solution)/shard_map/stack | solution.py:320
  137.5 0.0 copy-start.5
  137.5 10.3 %copy.15 = bf16[1,512,2,2560]{3,2,1,0:T(2,128)(2,1)} copy(bf16[1,512,2,2560]{3,1,2,0:T(8,128)(2,1)} %pad_maximum_fusion) | data formatting | bytes 10485760
  147.8 0.0 copy-done.5
  147.8 0.0 copy-start.4
  147.8 0.8 copy.27
  148.7 0.5 copy-done.4
  149.1 0.8 copy.28
  (2 shorter events, 0.0 us)
Async XLA Ops:
  68.0 3.5 %copy-start = (bf16[1,512,2,2560]{3,2,1,0:T(2,128)(2,1)S(1)}, bf16[1,512,2,2560]{3,2,1,0:T(2,128)(2,1)}, u32[]{:S(2)}) copy-start(bf16[1,512,2,2560]{3,2,1,0:T(2,128)(2,1)} %param.15) | copy-start | bytes 15728644
  80.1 1.4 copy-start.7
  81.5 2.2 %copy-start.9 = (bf16[320,512]{1,0:T(8,128)(2,1)}, bf16[320,512]{1,0:T(8,128)(2,1)S(1)}, u32[]{:S(2)}) copy-start(bf16[320,512]{1,0:T(8,128)(2,1)S(1)} %fusion.18) | copy-start | bytes 983044
  83.7 44.6 %copy-start.1 = (bf16[1,128,2560]{2,1,0:T(8,128)(2,1)S(1)}, bf16[1,128,2560]{2,1,0:T(8,128)(2,1)}, u32[]{:S(2)}) copy-start(bf16[1,128,2560]{2,1,0:T(8,128)(2,1)} %param.8) | copy-start | bytes 1966084
  83.7 44.9 %copy-start.6 = (f32[2560]{0:T(1024)S(1)}, f32[2560]{0:T(1024)}, u32[]{:S(2)}) copy-start(f32[2560]{0:T(1024)} %param.12) | copy-start | bytes 30724
  128.4 1.9 %copy-start.2 = (bf16[1,128,2560]{2,1,0:T(8,128)(2,1)S(1)}, bf16[1,128,2560]{2,1,0:T(8,128)(2,1)}, u32[]{:S(2)}) copy-start(bf16[1,128,2560]{2,1,0:T(8,128)(2,1)} %param.9) | copy-start | bytes 1966084
  128.4 1.9 %copy-start.3 = (bf16[128,2560]{1,0:T(8,128)(2,1)S(1)}, bf16[128,2560]{1,0:T(8,128)(2,1)}, u32[]{:S(2)}) copy-start(bf16[128,2560]{1,0:T(8,128)(2,1)} %shard_map.113) | copy-start | bytes 1966084
  130.2 1.4 copy-start.8
  131.6 1.6 %copy-start.10 = (bf16[320,512]{1,0:T(8,128)(2,1)S(1)}, bf16[320,512]{1,0:T(8,128)(2,1)}, u32[]{:S(2)}) copy-start(bf16[320,512]{1,0:T(8,128)(2,1)} %copy-done.9) | copy-start | bytes 983044
  137.5 10.3 %copy-start.5 = (bf16[128,2560]{1,0:T(8,128)(2,1)S(1)}, bf16[128,2560]{1,0:T(8,128)(2,1)}, u32[]{:S(2)}) copy-start(bf16[128,2560]{1,0:T(8,128)(2,1)} %get-tuple-element.18) | copy-start | bytes 1966084
  147.8 1.3 copy-start.4

commit v3 on v2

--- a/solution.py
+++ b/solution.py
@@ -73,8 +73,8 @@
 
 
 def dispatch_kernel(
-    ctx_count, experts, normed, upstream, keys, values, sends, stats,
-    got, keys_grad, values_grad, query_grad,
+    ctx_count, experts, normed, upstream, keys, values, sends, stats, weights,
+    got, keys_grad, values_grad, query_grad, w_in, w_out,
     stats_all, merged, direct_sem, forward_sem, got_sem, stats_send, stats_got,
 ):
     c, e = lax.axis_index("ctx"), lax.axis_index("exp")
@@ -103,14 +103,17 @@
             device_id={"ctx": lax.rem(c + d, ctx_count), "exp": e}, device_id_type=MESH,
         )
 
-    def goes(d):
-        return (lax.rem(e, ctx_count) == c) | (lax.rem(e + d, experts) // 2 == e // 2)
+    def carries(t, s):
+        return lax.rem(s + t * (ctx_count // 2), ctx_count) == c
+
+    def goes(t, d):
+        return carries(t, e) | (lax.rem(e + d, experts) // 2 == e // 2)
 
     for d in range(1, ctx_count):
         stats_copy(d).start()
     for t in range(2):
         for d in range(1, experts):
-            @pl.when(goes(d))
+            @pl.when(goes(t, d))
             def _():
                 direct_copy(t, d).start()
     for t in range(2):
@@ -142,7 +145,7 @@
         query_grad[:, cols] = (dot(score_grad, k, 0, 0) * HEAD ** (-0.5)).astype(BF16)
         return carry
 
-    lax.fori_loop(0, HEADS, one, 0)
+    lax.fori_loop(0, HEADS // 4, one, 0)
 
     def got_copy(t, s):
         return pltpu.make_async_remote_copy(
@@ -153,26 +156,43 @@
 
     for t in range(2):
         for s in range(experts):
-            @pl.when((s % ctx_count == c) & (s // 2 != e // 2))
+            @pl.when(carries(t, s) & (s // 2 != e // 2))
             def _():
                 got_copy(t, s).wait_recv()
                 for d in range(1, ctx_count):
                     forward_copy(t, s, d).start()
+        if t == 0:
+            lax.fori_loop(HEADS // 4, HEADS // 2, one, 0)
+    lax.fori_loop(HEADS // 2, HEADS, one, 0)
+    chunk = 64
+
+    def split(i, carry):
+        at = pl.ds(pl.multiple_of(i * chunk, chunk), chunk)
+        w_in[at, :] = weights[at, 0, :]
+        w_out[at, :] = weights[at, 1, :]
+        return carry
+
+    lax.fori_loop(0, weights.shape[0] // chunk, split, 0)
     for t in range(2):
         for s in range(experts):
-            @pl.when((s != e) & ((s % ctx_count != c) | (s // 2 == e // 2)))
+            @pl.when((s != e) & (jnp.logical_not(carries(t, s)) | (s // 2 == e // 2)))
             def _():
                 got_copy(t, s).wait_recv()
     for t in range(2):
         for s in range(experts):
-            @pl.when((s % ctx_count == c) & (s // 2 != e // 2))
+            @pl.when(carries(t, s) & (s // 2 != e // 2))
             def _():
                 for d in range(1, ctx_count):
                     forward_copy(t, s, d).wait_send()
         for d in range(1, experts):
-            @pl.when(goes(d))
+            @pl.when(goes(t, d))
             def _():
                 direct_copy(t, d).wait_send()
+
+
+def weights_kernel(pre_grad, activ, rows, douts, grad):
+    grad[:, 0, :] = dot(pre_grad[...], rows[...], 0, 0).astype(BF16)
+    grad[:, 1, :] = dot(activ[...], douts[...], 0, 0).astype(BF16)
 
 
 def return_kernel(
@@ -267,6 +287,7 @@
         (5 * TOP * tokens + 4 * expert_count * ctx_count - 1) // (4 * expert_count * ctx_count)
     )
     upstream = out_grad[0]
+    hidden = expert_weights.shape[1]
     vmem = pl.BlockSpec(memory_space=pltpu.VMEM)
     shape = jax.ShapeDtypeStruct
     dma = pltpu.SemaphoreType.DMA
@@ -282,16 +303,18 @@
         out_specs=(vmem,) * 4,
         compiler_params=pltpu.CompilerParams(vmem_limit_bytes=VMEM_LIMIT),
     )(states[0], upstream, doc_keys[0], doc_values[0], norm_gain[None], expert_ids[0].T, gate_values[0].T)
-    got, keys_grad, values_grad, query_grad = pl.pallas_call(
+    got, keys_grad, values_grad, query_grad, w_in, w_out = pl.pallas_call(
         functools.partial(dispatch_kernel, ctx_count, expert_count),
         out_shape=(
             shape((2, expert_count, capacity, model_width), BF16),
             shape((key_count, model_width), BF16),
             shape((key_count, model_width), BF16),
             shape((tokens, model_width), BF16),
-        ),
-        in_specs=[vmem] * 6,
-        out_specs=(vmem,) * 4,
+            shape((hidden, model_width), BF16),
+            shape((hidden, model_width), BF16),
+        ),
+        in_specs=[vmem] * 7,
+        out_specs=(vmem,) * 6,
         scratch_shapes=[
             pltpu.VMEM((ctx_count - 1, 3, HEADS, tokens), F32),
             pltpu.VMEM((3, HEADS, tokens), F32),
@@ -304,20 +327,26 @@
         compiler_params=pltpu.CompilerParams(
             vmem_limit_bytes=VMEM_LIMIT, collective_id=0, has_side_effects=True
         ),
-    )(normed, upstream, doc_keys[0], doc_values[0], sends, stats)
+    )(normed, upstream, doc_keys[0], doc_values[0], sends, stats, expert_weights[0])
     slot_rows = expert_count * capacity
     rows = got[0].reshape(slot_rows, model_width)
     douts = got[1].reshape(slot_rows, model_width)
-    w_in = expert_weights[0, :, 0, :]
-    w_out = expert_weights[0, :, 1, :]
     pre = jnp.einsum("sd,hd->sh", rows, w_in, preferred_element_type=jnp.float32)
     activ, pull = jax.vjp(jax.nn.gelu, pre)
     activ_low = activ.astype(jnp.bfloat16)
     act_grad = jnp.einsum("sd,hd->sh", douts, w_out, preferred_element_type=jnp.float32)
     pre_grad = pull(act_grad)[0].astype(jnp.bfloat16)
-    grad_in = jnp.einsum("sh,sd->hd", pre_grad, rows, preferred_element_type=jnp.float32)
-    grad_proj = jnp.einsum("sh,sd->hd", activ_low, douts, preferred_element_type=jnp.float32)
-    weights_grad = jnp.stack([grad_in, grad_proj], axis=1).astype(jnp.bfloat16)[None]
+    block = min(hidden, 128)
+    hidden_spec = pl.BlockSpec((slot_rows, block), lambda i: (0, i))
+    rows_spec = pl.BlockSpec((slot_rows, model_width), lambda i: (0, 0))
+    weights_grad = pl.pallas_call(
+        weights_kernel,
+        grid=(hidden // block,),
+        out_shape=shape((hidden, 2, model_width), BF16),
+        in_specs=[hidden_spec, hidden_spec, rows_spec, rows_spec],
+        out_specs=pl.BlockSpec((block, 2, model_width), lambda i: (i, 0, 0)),
+        compiler_params=pltpu.CompilerParams(vmem_limit_bytes=VMEM_LIMIT),
+    )(pre_grad, activ_low, rows, douts)[None]
     partial_rows = jnp.einsum("sh,hd->sd", pre_grad, w_in, preferred_element_type=jnp.float32)
     tiles = model_width // HEAD
     width = HEAD * max(

time: 150 us -> 133 us (0.89)
  local copies, waits for them, and re-layouts: 24.9 us -> 7.17 us
  Pallas kernels: 111 us -> 116 us
  other arithmetic: 5.89 us -> 3.15 us
  matrix products: 7.74 us -> 5.5 us
    unnamed x25 -> x26, local copies, waits for them, and re-layouts: 13.7 us -> 3.55 us
    slice x1 -> x0, local copies, waits for them, and re-layouts: 7.6 us -> none  [on_device(): w_out = expert_weights[0, :, 1, :]]
    pallas_call x0 -> x1, Pallas kernels: none -> 7.37 us  [on_device(): pl.pallas_call(weights_kernel, grid=(hidden // block,), out_shape=shape((...]
    pallas_call x1, Pallas kernels: 59.2 us -> 54.8 us  [on_device(): pl.pallas_call(functools.partial(dispatch_kernel, ctx_count, expert_count...]
    dot_general x2 -> x0, matrix products: 3.15 us -> none  [the longest x1 1.61 us: on_device(): jnp.einsum('sh,sd->hd', activ_low, douts, preferred_element_type=jnp.floa...]
    another operation x1 -> x0, other arithmetic: 2.75 us -> none  [on_device(): jnp.stack([grad_in, grad_proj], axis=1).astype(jnp.bfloat16)[None]]
    pallas_call x1, Pallas kernels: 44.6 us -> 47.3 us  [on_device(): pl.pallas_call(functools.partial(return_kernel, ctx_count, expert_count,...]
where the time goes in v3:
time: 133 us
  Pallas kernels  116 us (87%)
  local copies, waits for them, and re-layouts  7.17 us (5%)
  matrix products  5.5 us (4%)
  other arithmetic  3.15 us (2%)
    pallas_call x1, Pallas kernels, on_device(): pl.pallas_call(functools.partial(dispatch_kernel, ctx_count, expert_count...  54.8 us
    pallas_call x1, Pallas kernels, on_device(): pl.pallas_call(functools.partial(return_kernel, ctx_count, expert_count,...  47.3 us
    pallas_call x1, Pallas kernels, on_device(): pl.pallas_call(weights_kernel, grid=(hidden // block,), out_shape=shape((...  7.37 us
    pallas_call x1, Pallas kernels, on_device(): pl.pallas_call(functools.partial(front_kernel, expert_count, capacity), o...  6.87 us
    unnamed x26, local copies, waits for them, and re-layouts  3.55 us

profile of v3, /device:TPU:0, one launch (start us, length us, event | category | flops | bytes accessed | tf_op | source)
XLA Modules:
  0.0 132.9 jit_solution(14724674657302124236)
XLA Ops:
  0.6 1.3 broadcast_in_dim.18.gain
  1.9 6.9 %shard_map.111 = (bf16[128,2560]{1,0:T(8,128)(2,1)}, bf16[2,8,40,2560]{3,2,1,0:T(8,128)(2,1)}, bf16[8,40,128]{2,1,0:T(8,128)(2,1)}, f32[3,20,128]{2,1,0:T(8,128)}) custom-call(bf16[128,2560]{1,0:T(8,128)(2,1)} %bitcast.29, bf16[128,2560]{1,0:T(8,128)(2,1)} %bitcast.34, bf16[128,2560]{1,0:T(8,128)(2,1)} %bitcast.38, bf16[128,2560]{1,0:T(8,128)(2,1)} %bitcast.40, ...), custom_call_target="tpu_custom_call" | custom-call | tf_op jit(solution)/shard_map/pallas_call | solution.py:294
  8.8 54.8 %shard_map.112 = (bf16[2,8,40,2560]{3,2,1,0:T(8,128)(2,1)}, bf16[128,2560]{1,0:T(8,128)(2,1)}, bf16[128,2560]{1,0:T(8,128)(2,1)}, bf16[128,2560]{1,0:T(8,128)(2,...) custom-call(bf16[128,2560]{1,0:T(8,128)(2,1)} %get-tuple-element.14.normed, bf16[128,2560]{1,0:T(8,128)(2,1)} %bitcast.35, ...), custom_call_target="tpu_custom_call" | custom-call | tf_op jit(solution)/shard_map/pallas_call | solution.py:306
  63.6 0.0 copy-start.11
  63.6 2.3 %fusion.16 = (bf16[1,8,40,2560]{3,2,1,0:T(8,128)(2,1)S(1)}, bf16[1,8,40,2560]{3,2,1,0:T(8,128)(2,1)S(1)}) fusion(bf16[2,8,40,2560]{3,2,1,0:T(8,128)(2,1)} %get-tuple-element.17), kind=kLoop, calls=%fused_computation.25 | loop fusion | bytes 6553600 | tf_op jit(solution)/shard_map/slice | solution.py:333
  65.9 0.0 copy-start.1
  65.9 0.0 copy-start.2
  65.9 0.4 copy-done.11
  66.3 0.0 copy-start.9
  66.3 1.0 fusion.17
  67.4 0.0 copy-done.1
  67.4 0.2 copy-done.2
  67.6 1.2 copy-done.9
  68.8 2.3 %multiply_convert_fusion = (bf16[320,512]{1,0:T(8,128)(2,1)}, bf16[320,512]{1,0:T(8,128)(2,1)}) fusion(f32[320,512]{1,0:T(8,128)S(1)} %fusion.17, bf16[320,2560]{1,0:T(8,128)(2,1)S(1)} %bitcast.32, bf16[512,2560]{1,0:T(8,128)(2,1)S(1)} %copy-done.9), kind=kOutput, calls=%fused_computation.22 | convolution fusion | flops 842465280 | bytes 5570560 | tf_op jit(solution)/shard_map/sd,hd->sh/dot_general | solution.py:334
  71.1 0.0 copy-start.7
  71.1 0.0 copy-start.10
  71.1 7.4 %shard_map.114 = bf16[512,2,2560]{2,1,0:T(2,128)(2,1)} custom-call(bf16[320,512]{1,0:T(8,128)(2,1)} %get-tuple-element.27.pre_grad, bf16[320,512]{1,0:T(8,128)(2,1)} %get-tuple-element.26.activ, bf16[320,2560]{1,0:T(8,128)(2,1)} %bitcast.33, bf16[320,2560]{1,0:T(8,128)(2,1)} %bitcast.31), custom_call_target="tpu_custom_call" | custom-call | tf_op jit(solution)/shard_map/pallas_call | solution.py:342
  78.5 0.0 copy-done.7
  78.5 0.0 copy-done.10
  78.5 2.2 %convolution_convert_fusion = bf16[320,2560]{1,0:T(8,128)(2,1)} fusion(bf16[320,512]{1,0:T(8,128)(2,1)S(1)} %copy-done.7, bf16[512,2560]{1,0:T(8,128)(2,1)S(1)} %copy-done.10), kind=kOutput, calls=%fused_computation | convolution fusion | flops 839680000 | bytes 4587520 | tf_op jit(solution)/shard_map/sh,hd->sd/dot_general | solution.py:350
  80.7 0.0 copy-start
  80.7 0.0 copy-start.8
  80.7 47.3 %shard_map.113 = bf16[128,2560]{1,0:T(8,128)(2,1)} custom-call(bf16[8,40,2560]{2,1,0:T(8,128)(2,1)} %bitcast.42, bf16[128,2560]{1,0:T(8,128)(2,1)} %get-tuple-element.20.query_grad, bf16[8,40,128]{2,1,0:T(8,128)(2,1)} %get-tuple-element.21.select), custom_call_target="tpu_custom_call" | custom-call | tf_op jit(solution)/shard_map/pallas_call | solution.py:356
  128.0 0.0 copy-done
  128.1 0.0 copy-start.3
  128.1 0.0 copy-start.4
  128.1 0.2 fusion.7
  128.3 0.0 copy-done.8
  128.3 1.6 %fusion.2 = f32[128]{0:T(128)S(1)} fusion(bf16[128,2560]{1,0:T(8,128)(2,1)} %shard_map.113, f32[2560]{0:T(1024)S(1)} %copy-done.8, f32[128]{0:T(128)S(1)} %add_rsqrt_fusion, bf16[1,128,2560]{2,1,0:T(8,128)(2,1)S(1)} %copy-done), kind=kLoop, calls=%fused_computation.5 | loop fusion | flops 1965952 | bytes 1321984 | tf_op jit(solution)/shard_map/reduce_sum | solution.py:387
  129.9 0.0 copy-start.6
  129.9 0.0 copy-done.3
  129.9 0.0 copy-done.4
  129.9 0.0 copy-start.5
  130.0 1.3 fusion.15
  131.3 0.0 copy-done.6
  131.3 0.8 copy.14
  132.1 0.0 copy-done.5
  132.1 0.8 copy.15
  (2 shorter events, 0.0 us)
Async XLA Ops:
  63.6 2.7 %copy-start.11 = (bf16[512,2560]{1,0:T(8,128)(2,1)S(1)}, bf16[512,2560]{1,0:T(8,128)(2,1)}, u32[]{:S(2)}) copy-start(bf16[512,2560]{1,0:T(8,128)(2,1)} %get-tuple-element.18) | copy-start | bytes 7864324
  65.9 1.5 %copy-start.1 = (bf16[1,8,40,2560]{3,2,1,0:T(8,128)(2,1)}, bf16[1,8,40,2560]{3,2,1,0:T(8,128)(2,1)S(1)}, u32[]{:S(2)}) copy-start(bf16[1,8,40,2560]{3,2,1,0:T(8,128)(2,1)S(1)} %get-tuple-element.24) | copy-start | bytes 4915204
  65.9 1.7 %copy-start.2 = (bf16[1,8,40,2560]{3,2,1,0:T(8,128)(2,1)}, bf16[1,8,40,2560]{3,2,1,0:T(8,128)(2,1)S(1)}, u32[]{:S(2)}) copy-start(bf16[1,8,40,2560]{3,2,1,0:T(8,128)(2,1)S(1)} %get-tuple-element.25) | copy-start | bytes 4915204
  66.3 2.5 %copy-start.9 = (bf16[512,2560]{1,0:T(8,128)(2,1)S(1)}, bf16[512,2560]{1,0:T(8,128)(2,1)}, u32[]{:S(2)}) copy-start(bf16[512,2560]{1,0:T(8,128)(2,1)} %get-tuple-element.19) | copy-start | bytes 7864324
  71.1 7.4 %copy-start.7 = (bf16[320,512]{1,0:T(8,128)(2,1)S(1)}, bf16[320,512]{1,0:T(8,128)(2,1)}, u32[]{:S(2)}) copy-start(bf16[320,512]{1,0:T(8,128)(2,1)} %get-tuple-element.27.pre_grad) | copy-start | bytes 983044
  71.1 7.4 %copy-start.10 = (bf16[512,2560]{1,0:T(8,128)(2,1)S(1)}, bf16[512,2560]{1,0:T(8,128)(2,1)}, u32[]{:S(2)}) copy-start(bf16[512,2560]{1,0:T(8,128)(2,1)} %get-tuple-element.19) | copy-start | bytes 7864324
  80.7 47.4 %copy-start = (bf16[1,128,2560]{2,1,0:T(8,128)(2,1)S(1)}, bf16[1,128,2560]{2,1,0:T(8,128)(2,1)}, u32[]{:S(2)}) copy-start(bf16[1,128,2560]{2,1,0:T(8,128)(2,1)} %param.8) | copy-start | bytes 1966084
  80.7 47.6 %copy-start.8 = (f32[2560]{0:T(1024)S(1)}, f32[2560]{0:T(1024)}, u32[]{:S(2)}) copy-start(f32[2560]{0:T(1024)} %param.12) | copy-start | bytes 30724
  128.1 1.9 %copy-start.3 = (bf16[1,128,2560]{2,1,0:T(8,128)(2,1)S(1)}, bf16[1,128,2560]{2,1,0:T(8,128)(2,1)}, u32[]{:S(2)}) copy-start(bf16[1,128,2560]{2,1,0:T(8,128)(2,1)} %param.9) | copy-start | bytes 1966084
  128.1 1.9 %copy-start.4 = (bf16[128,2560]{1,0:T(8,128)(2,1)S(1)}, bf16[128,2560]{1,0:T(8,128)(2,1)}, u32[]{:S(2)}) copy-start(bf16[128,2560]{1,0:T(8,128)(2,1)} %shard_map.113) | copy-start | bytes 1966084
  129.9 1.4 %copy-start.6 = (bf16[128,2560]{1,0:T(8,128)(2,1)S(1)}, bf16[128,2560]{1,0:T(8,128)(2,1)}, u32[]{:S(2)}) copy-start(bf16[128,2560]{1,0:T(8,128)(2,1)} %get-tuple-element.22) | copy-start | bytes 1966084
  129.9 2.2 %copy-start.5 = (bf16[128,2560]{1,0:T(8,128)(2,1)S(1)}, bf16[128,2560]{1,0:T(8,128)(2,1)}, u32[]{:S(2)}) copy-start(bf16[128,2560]{1,0:T(8,128)(2,1)} %get-tuple-element.23) | copy-start | bytes 1966084

commit v4 on v3

--- a/solution.py
+++ b/solution.py
@@ -26,11 +26,11 @@
     return pl.ds(pl.multiple_of(h * HEAD, HEAD), HEAD)
 
 
-def front_kernel(experts, capacity, states, upstream, keys, values, gain, ids, gates, normed, sends, select, stats):
+def front_kernel(experts, capacity, states, upstream, gain, ids, gates, normed, sends, select):
     tokens = states.shape[0]
     inputs = states[...].astype(F32)
     inverse = lax.rsqrt(jnp.mean(inputs * inputs, axis=-1, keepdims=True) + EPSILON)
-    normed[...] = (inputs * inverse * gain[...]).astype(BF16)
+    normed[...] = (inputs * inverse * gain[...][None]).astype(BF16)
     expert = lax.broadcasted_iota(jnp.int32, (experts, tokens), 0)
     first, second = ids[0:1, :] == expert, ids[1:2, :] == expert
     chosen = jnp.where(first | second, 1.0, 0.0)
@@ -49,19 +49,6 @@
         sends[0, e] = dot(picked, normed[...], 1, 0).astype(BF16)
         sends[1, e] = (dot(picked, upstream[...], 1, 0) * slot_gate).astype(BF16)
 
-    def one(h, carry):
-        cols = head_cols(h)
-        scores = dot(keys[:, cols], normed[:, cols], 1, 1) * HEAD ** (-0.5)
-        peak = jnp.max(scores, axis=0, keepdims=True)
-        weights = jnp.exp(scores - peak)
-        slopes = dot(values[:, cols], upstream[:, cols], 1, 1)
-        stats[0, pl.ds(h, 1), :] = peak
-        stats[1, pl.ds(h, 1), :] = jnp.sum(weights, axis=0, keepdims=True)
-        stats[2, pl.ds(h, 1), :] = jnp.sum(weights * slopes, axis=0, keepdims=True)
-        return carry
-
-    lax.fori_loop(0, HEADS, one, 0, unroll=4)
-
 
 def entry_barrier(ctx_count, experts, c, e):
     barrier = pltpu.get_barrier_semaphore()
@@ -73,11 +60,12 @@
 
 
 def dispatch_kernel(
-    ctx_count, experts, normed, upstream, keys, values, sends, stats, weights,
-    got, keys_grad, values_grad, query_grad, w_in, w_out,
-    stats_all, merged, direct_sem, forward_sem, got_sem, stats_send, stats_got,
+    ctx_count, experts, normed, upstream, keys, values, sends, weights,
+    got_rows, got_grads, keys_grad, values_grad, query_grad, w_in, w_out,
+    stats, stats_all, merged, direct_sem, forward_sem, got_sem, stats_send, stats_got,
 ):
     c, e = lax.axis_index("ctx"), lax.axis_index("exp")
+    got = (got_rows, got_grads)
     entry_barrier(ctx_count, experts, c, e)
 
     def stats_copy(d):
@@ -91,14 +79,14 @@
     def direct_copy(t, d):
         to = lax.rem(e + d, experts)
         return pltpu.make_async_remote_copy(
-            src_ref=sends.at[t, to], dst_ref=got.at[t, e],
+            src_ref=sends.at[t, to], dst_ref=got[t].at[e],
             send_sem=direct_sem.at[t, d], recv_sem=got_sem.at[t, e],
             device_id={"ctx": c, "exp": to}, device_id_type=MESH,
         )
 
     def forward_copy(t, s, d):
         return pltpu.make_async_remote_copy(
-            src_ref=got.at[t, s], dst_ref=got.at[t, s],
+            src_ref=got[t].at[s], dst_ref=got[t].at[s],
             send_sem=forward_sem.at[t, s, d - 1], recv_sem=got_sem.at[t, s],
             device_id={"ctx": lax.rem(c + d, ctx_count), "exp": e}, device_id_type=MESH,
         )
@@ -109,15 +97,28 @@
     def goes(t, d):
         return carries(t, e) | (lax.rem(e + d, experts) // 2 == e // 2)
 
-    for d in range(1, ctx_count):
-        stats_copy(d).start()
     for t in range(2):
         for d in range(1, experts):
             @pl.when(goes(t, d))
             def _():
                 direct_copy(t, d).start()
+
+    def local(h, carry):
+        cols = head_cols(h)
+        scores = dot(keys[:, cols], normed[:, cols], 1, 1) * HEAD ** (-0.5)
+        peak = jnp.max(scores, axis=0, keepdims=True)
+        weight = jnp.exp(scores - peak)
+        slopes = dot(values[:, cols], upstream[:, cols], 1, 1)
+        stats[0, pl.ds(h, 1), :] = peak
+        stats[1, pl.ds(h, 1), :] = jnp.sum(weight, axis=0, keepdims=True)
+        stats[2, pl.ds(h, 1), :] = jnp.sum(weight * slopes, axis=0, keepdims=True)
+        return carry
+
+    lax.fori_loop(0, HEADS, local, 0, unroll=4)
     for t in range(2):
-        got[t, e] = sends[t, e]
+        got[t][e] = sends[t, e]
+    for d in range(1, ctx_count):
+        stats_copy(d).start()
     for d in range(1, ctx_count):
         stats_copy(d).wait()
     peak = stats[0]
@@ -149,7 +150,7 @@
 
     def got_copy(t, s):
         return pltpu.make_async_remote_copy(
-            src_ref=got.at[t, s], dst_ref=got.at[t, s],
+            src_ref=got[t].at[s], dst_ref=got[t].at[s],
             send_sem=direct_sem.at[t, 0], recv_sem=got_sem.at[t, s],
             device_id={"ctx": c, "exp": lax.rem(e + 1, experts)}, device_id_type=MESH,
         )
@@ -291,31 +292,32 @@
     vmem = pl.BlockSpec(memory_space=pltpu.VMEM)
     shape = jax.ShapeDtypeStruct
     dma = pltpu.SemaphoreType.DMA
-    normed, sends, select, stats = pl.pallas_call(
+    normed, sends, select = pl.pallas_call(
         functools.partial(front_kernel, expert_count, capacity),
         out_shape=(
             shape((tokens, model_width), BF16),
             shape((2, expert_count, capacity, model_width), BF16),
             shape((expert_count, capacity, tokens), BF16),
-            shape((3, HEADS, tokens), F32),
-        ),
-        in_specs=[vmem] * 7,
-        out_specs=(vmem,) * 4,
+        ),
+        in_specs=[vmem] * 5,
+        out_specs=(vmem,) * 3,
         compiler_params=pltpu.CompilerParams(vmem_limit_bytes=VMEM_LIMIT),
-    )(states[0], upstream, doc_keys[0], doc_values[0], norm_gain[None], expert_ids[0].T, gate_values[0].T)
-    got, keys_grad, values_grad, query_grad, w_in, w_out = pl.pallas_call(
+    )(states[0], upstream, norm_gain, expert_ids[0].T, gate_values[0].T)
+    got_rows, got_grads, keys_grad, values_grad, query_grad, w_in, w_out = pl.pallas_call(
         functools.partial(dispatch_kernel, ctx_count, expert_count),
         out_shape=(
-            shape((2, expert_count, capacity, model_width), BF16),
+            shape((expert_count, capacity, model_width), BF16),
+            shape((expert_count, capacity, model_width), BF16),
             shape((key_count, model_width), BF16),
             shape((key_count, model_width), BF16),
             shape((tokens, model_width), BF16),
             shape((hidden, model_width), BF16),
             shape((hidden, model_width), BF16),
         ),
-        in_specs=[vmem] * 7,
-        out_specs=(vmem,) * 6,
+        in_specs=[vmem] * 6,
+        out_specs=(vmem,) * 7,
         scratch_shapes=[
+            pltpu.VMEM((3, HEADS, tokens), F32),
             pltpu.VMEM((ctx_count - 1, 3, HEADS, tokens), F32),
             pltpu.VMEM((3, HEADS, tokens), F32),
             dma((2, expert_count)),
@@ -327,10 +329,10 @@
         compiler_params=pltpu.CompilerParams(
             vmem_limit_bytes=VMEM_LIMIT, collective_id=0, has_side_effects=True
         ),
-    )(normed, upstream, doc_keys[0], doc_values[0], sends, stats, expert_weights[0])
+    )(normed, upstream, doc_keys[0], doc_values[0], sends, expert_weights[0])
     slot_rows = expert_count * capacity
-    rows = got[0].reshape(slot_rows, model_width)
-    douts = got[1].reshape(slot_rows, model_width)
+    rows = got_rows.reshape(slot_rows, model_width)
+    douts = got_grads.reshape(slot_rows, model_width)
     pre = jnp.einsum("sd,hd->sh", rows, w_in, preferred_element_type=jnp.float32)
     activ, pull = jax.vjp(jax.nn.gelu, pre)
     activ_low = activ.astype(jnp.bfloat16)

time: 133 us -> 128 us (0.962)
  local copies, waits for them, and re-layouts: 7.17 us -> 1.78 us
  matrix products: 5.5 us -> 7.87 us
  Pallas kernels: 116 us -> 114 us
    dot_general x1, matrix products: 1.03 us -> 3.42 us  [on_device(): jnp.einsum('sd,hd->sh', douts, w_out, preferred_element_type=jnp.float32)]
    slice x1 -> x0, local copies, waits for them, and re-layouts: 2.3 us -> none  [on_device(): douts = got[1].reshape(slot_rows, model_width)]
    pallas_call x1, Pallas kernels: 6.87 us -> 4.79 us  [on_device(): pl.pallas_call(functools.partial(front_kernel, expert_count, capacity), o...]
    unnamed x26 -> x22, local copies, waits for them, and re-layouts: 3.55 us -> 1.78 us
where the time goes in v4:
time: 128 us
  Pallas kernels  114 us (89%)
  matrix products  7.87 us (6%)
  other arithmetic  3.15 us (2%)
  local copies, waits for them, and re-layouts  1.78 us (1%)
    pallas_call x1, Pallas kernels, on_device(): pl.pallas_call(functools.partial(dispatch_kernel, ctx_count, expert_count...  54.9 us
    pallas_call x1, Pallas kernels, on_device(): pl.pallas_call(functools.partial(return_kernel, ctx_count, expert_count,...  47.3 us
    pallas_call x1, Pallas kernels, on_device(): pl.pallas_call(weights_kernel, grid=(hidden // block,), out_shape=shape((...  7.38 us
    pallas_call x1, Pallas kernels, on_device(): pl.pallas_call(functools.partial(front_kernel, expert_count, capacity), o...  4.79 us
    dot_general x1, matrix products, on_device(): jnp.einsum('sd,hd->sh', douts, w_out, preferred_element_type=jnp.float32)  3.42 us

profile of v4, /device:TPU:0, one launch (start us, length us, event | category | flops | bytes accessed | tf_op | source)
XLA Modules:
  0.0 128.0 jit_solution(14708450520185027813)
XLA Ops:
  0.6 4.8 %shard_map.111 = (bf16[128,2560]{1,0:T(8,128)(2,1)}, bf16[2,8,40,2560]{3,2,1,0:T(8,128)(2,1)}, bf16[8,40,128]{2,1,0:T(8,128)(2,1)}) custom-call(bf16[128,2560]{1,0:T(8,128)(2,1)} %bitcast.29, bf16[128,2560]{1,0:T(8,128)(2,1)} %bitcast.30, f32[2560]{0:T(1024)} %gain.1, s32[2,128]{1,0:T(2,128)} %bitcast.43, f32[2,128]{1,0:T(2,128)} %bitcast.44), custom_call_target="tpu_custom_call" | custom-call | tf_op jit(solution)/shard_map/pallas_call | solution.py:295
  5.4 54.9 %shard_map.112 = (bf16[8,40,2560]{2,1,0:T(8,128)(2,1)}, bf16[8,40,2560]{2,1,0:T(8,128)(2,1)}, bf16[128,2560]{1,0:T(8,128)(2,1)}, bf16[128,2560]{1,0:T(8,128)(2,1...) custom-call(bf16[128,2560]{1,0:T(8,128)(2,1)} %get-tuple-element.14.normed, ...), custom_call_target="tpu_custom_call" | custom-call | tf_op jit(solution)/shard_map/pallas_call | solution.py:306
  60.3 0.0 copy-start.3
  60.3 0.0 copy-start.8
  60.3 3.4 %fusion.16 = f32[320,512]{1,0:T(8,128)S(1)} fusion(bf16[320,2560]{1,0:T(8,128)(2,1)} %bitcast.37, bf16[512,2560]{1,0:T(8,128)(2,1)} %get-tuple-element.17), kind=kOutput, calls=%fused_computation.25 | convolution fusion | flops 838860800 | bytes 4915200 | tf_op jit(solution)/shard_map/sd,hd->sh/dot_general | solution.py:339
  63.8 0.0 copy-done.3
  63.8 0.1 copy-done.8
  63.8 2.3 %multiply_convert_fusion = (bf16[320,512]{1,0:T(8,128)(2,1)}, bf16[320,512]{1,0:T(8,128)(2,1)}) fusion(f32[320,512]{1,0:T(8,128)S(1)} %fusion.16, bf16[320,2560]{1,0:T(8,128)(2,1)S(1)} %bitcast.36, bf16[512,2560]{1,0:T(8,128)(2,1)S(1)} %copy-done.8), kind=kOutput, calls=%fused_computation.22 | convolution fusion | flops 842465280 | bytes 5570560 | tf_op jit(solution)/shard_map/sd,hd->sh/dot_general | solution.py:336
  66.1 0.0 copy-start.6
  66.1 0.0 copy-start.9
  66.1 7.4 %shard_map.114 = bf16[512,2,2560]{2,1,0:T(2,128)(2,1)} custom-call(bf16[320,512]{1,0:T(8,128)(2,1)} %get-tuple-element.25.pre_grad, bf16[320,512]{1,0:T(8,128)(2,1)} %get-tuple-element.24.activ, bf16[320,2560]{1,0:T(8,128)(2,1)} %bitcast.35, bf16[320,2560]{1,0:T(8,128)(2,1)} %bitcast.38), custom_call_target="tpu_custom_call" | custom-call | tf_op jit(solution)/shard_map/pallas_call | solution.py:344
  73.5 0.0 copy-done.6
  73.5 0.0 copy-done.9
  73.5 2.2 %convolution_convert_fusion = bf16[320,2560]{1,0:T(8,128)(2,1)} fusion(bf16[320,512]{1,0:T(8,128)(2,1)S(1)} %copy-done.6, bf16[512,2560]{1,0:T(8,128)(2,1)S(1)} %copy-done.9), kind=kOutput, calls=%fused_computation | convolution fusion | flops 839680000 | bytes 4587520 | tf_op jit(solution)/shard_map/sh,hd->sd/dot_general | solution.py:352
  75.7 0.0 copy-start
  75.7 0.0 copy-start.7
  75.7 47.3 %shard_map.113 = bf16[128,2560]{1,0:T(8,128)(2,1)} custom-call(bf16[8,40,2560]{2,1,0:T(8,128)(2,1)} %bitcast.34, bf16[128,2560]{1,0:T(8,128)(2,1)} %get-tuple-element.20.query_grad, bf16[8,40,128]{2,1,0:T(8,128)(2,1)} %get-tuple-element.21.select), custom_call_target="tpu_custom_call" | custom-call | tf_op jit(solution)/shard_map/pallas_call | solution.py:358
  123.1 0.0 copy-done
  123.1 0.0 copy-start.1
  123.1 0.0 copy-start.2
  123.1 0.2 fusion.7
  123.3 0.0 copy-done.7
  123.3 1.6 %fusion.2 = f32[128]{0:T(128)S(1)} fusion(bf16[128,2560]{1,0:T(8,128)(2,1)} %shard_map.113, f32[2560]{0:T(1024)S(1)} %copy-done.7, f32[128]{0:T(128)S(1)} %add_rsqrt_fusion, bf16[1,128,2560]{2,1,0:T(8,128)(2,1)S(1)} %copy-done), kind=kLoop, calls=%fused_computation.5 | loop fusion | flops 1965952 | bytes 1321984 | tf_op jit(solution)/shard_map/reduce_sum | solution.py:389
  124.9 0.0 copy-start.5
  124.9 0.0 copy-done.1
  125.0 0.0 copy-done.2
  125.0 0.0 copy-start.4
  125.0 1.3 %fusion.15 = bf16[1,128,2560]{2,1,0:T(8,128)(2,1)} fusion(bf16[128,2560]{1,0:T(8,128)(2,1)S(1)} %copy-done.1, f32[128]{0:T(128)S(1)} %broadcast_multiply_fusion, f32[2560]{0:T(1024)S(1)} %copy-done.7, f32[128]{0:T(128)S(1)} %add_rsqrt_fusion, bf16[1,128,2560]{2,1,0:T(8,128)(2,1)S(1)} %copy-done, bf16[1,128,2560]{2,1,0:T(8,128)(2,1)S(1)} %copy-done.2), kind=kLoop, calls=%fused_computation.21 | loop fusion | flops 3276800 | bytes 2632704 | tf_op jit(solution)/shard_map/broadcast_in_dim | solution.py:392
  126.3 0.0 copy-done.5
  126.3 0.8 copy.14
  127.1 0.0 copy-done.4
  127.1 0.8 copy.15
  (2 shorter events, 0.0 us)
Async XLA Ops:
  60.3 3.4 %copy-start.3 = (bf16[8,40,2560]{2,1,0:T(8,128)(2,1)S(1)}, bf16[8,40,2560]{2,1,0:T(8,128)(2,1)}, u32[]{:S(2)}) copy-start(bf16[8,40,2560]{2,1,0:T(8,128)(2,1)} %get-tuple-element.18) | copy-start | bytes 4915204
  60.3 3.5 %copy-start.8 = (bf16[512,2560]{1,0:T(8,128)(2,1)S(1)}, bf16[512,2560]{1,0:T(8,128)(2,1)}, u32[]{:S(2)}) copy-start(bf16[512,2560]{1,0:T(8,128)(2,1)} %get-tuple-element.19) | copy-start | bytes 7864324
  66.1 7.4 %copy-start.6 = (bf16[320,512]{1,0:T(8,128)(2,1)S(1)}, bf16[320,512]{1,0:T(8,128)(2,1)}, u32[]{:S(2)}) copy-start(bf16[320,512]{1,0:T(8,128)(2,1)} %get-tuple-element.25.pre_grad) | copy-start | bytes 983044
  66.1 7.4 %copy-start.9 = (bf16[512,2560]{1,0:T(8,128)(2,1)S(1)}, bf16[512,2560]{1,0:T(8,128)(2,1)}, u32[]{:S(2)}) copy-start(bf16[512,2560]{1,0:T(8,128)(2,1)} %get-tuple-element.19) | copy-start | bytes 7864324
  75.7 47.4 %copy-start = (bf16[1,128,2560]{2,1,0:T(8,128)(2,1)S(1)}, bf16[1,128,2560]{2,1,0:T(8,128)(2,1)}, u32[]{:S(2)}) copy-start(bf16[1,128,2560]{2,1,0:T(8,128)(2,1)} %param.8) | copy-start | bytes 1966084
  75.7 47.6 %copy-start.7 = (f32[2560]{0:T(1024)S(1)}, f32[2560]{0:T(1024)}, u32[]{:S(2)}) copy-start(f32[2560]{0:T(1024)} %gain.1) | copy-start | bytes 30724
  123.1 1.9 %copy-start.1 = (bf16[128,2560]{1,0:T(8,128)(2,1)S(1)}, bf16[128,2560]{1,0:T(8,128)(2,1)}, u32[]{:S(2)}) copy-start(bf16[128,2560]{1,0:T(8,128)(2,1)} %shard_map.113) | copy-start | bytes 1966084
  123.1 1.9 %copy-start.2 = (bf16[1,128,2560]{2,1,0:T(8,128)(2,1)S(1)}, bf16[1,128,2560]{2,1,0:T(8,128)(2,1)}, u32[]{:S(2)}) copy-start(bf16[1,128,2560]{2,1,0:T(8,128)(2,1)} %param.9) | copy-start | bytes 1966084
  124.9 1.4 %copy-start.5 = (bf16[128,2560]{1,0:T(8,128)(2,1)S(1)}, bf16[128,2560]{1,0:T(8,128)(2,1)}, u32[]{:S(2)}) copy-start(bf16[128,2560]{1,0:T(8,128)(2,1)} %get-tuple-element.22) | copy-start | bytes 1966084
  125.0 2.2 %copy-start.4 = (bf16[128,2560]{1,0:T(8,128)(2,1)S(1)}, bf16[128,2560]{1,0:T(8,128)(2,1)}, u32[]{:S(2)}) copy-start(bf16[128,2560]{1,0:T(8,128)(2,1)} %get-tuple-element.23) | copy-start | bytes 1966084
